TPU v7x, 32 devices: a whole 2x2x4 slice. The times are simulated.
32 devices in a mesh: ids: 8 (over z, x), mdl: 4 (over y, core).
Axes of the slice: x: 2, y: 2, z: 4, core: 2. Of those that a mesh axis runs over, the one named last changes fastest.
Arguments:
- hash_codes: int32 [32768, 1024], P('ids', 'mdl'), may hold values from 0 to 1023
- request_ids: int32 [64, 1024], P('ids'), may hold values from 0 to 32767, as said below
- request_counts: int32 [64], P('ids'), may hold values from 256 to 1024, as said below
- token_slots: int32 [65536], P('ids'), may hold values from 0 to 8191, as said below
- cotangent: bfloat16 [65536, 32], P('ids'), may hold values from -6 to 6
- weight_first: float32 [1024, 1800], P('ids', 'mdl'), may hold values from -0.1875 to 0.1875
- weight_second: float32 [1800, 1800], P(None, 'mdl'), may hold values from -0.125 to 0.125
- weight_final: float32 [1800, 32], P('mdl'), may hold values from -0.125 to 0.125
- norm_params: float32 [4, 1800], P(None, 'mdl')
- bias_final: float32 [32], replicated, may hold values from -0.5 to 0.5
- moment_first: float32 [1024, 1800], P('ids', 'mdl'), may hold values from -0.0007324219 to 0.0007324219
- square_first: float32 [1024, 1800], P('ids', 'mdl'), may hold values from 1.373291e-09 to 5.493164e-09
- moment_second: float32 [1800, 1800], P(None, 'mdl'), may hold values from -0.0007324219 to 0.0007324219
- square_second: float32 [1800, 1800], P(None, 'mdl'), may hold values from 1.373291e-09 to 5.493164e-09
- moment_final: float32 [1800, 32], P('mdl'), may hold values from -0.0048828125 to 0.0048828125
- square_final: float32 [1800, 32], P('mdl'), may hold values from 6.103516e-08 to 2.4414064e-07
- moment_norm: float32 [4, 1800], P(None, 'mdl'), may hold values from -0.001953125 to 0.001953125
- square_norm: float32 [4, 1800], P(None, 'mdl'), may hold values from 9e-09 to 3.6e-08
- moment_bias: float32 [32], replicated, may hold values from -0.03125 to 0.03125
- square_bias: float32 [32], replicated, may hold values from 2.5e-06 to 1e-05
Outputs:
- token_embed: bfloat16 [65536, 32], P('ids')
- momentum_first: float32 [1024, 1800], P('ids', 'mdl')
- variance_first: float32 [1024, 1800], P('ids', 'mdl')
- master_first: float32 [1024, 1800], P('ids', 'mdl')
- bfloat_first: bfloat16 [1024, 1800], P('ids', 'mdl')
- momentum_second: float32 [1800, 1800], P(None, 'mdl')
- variance_second: float32 [1800, 1800], P(None, 'mdl')
- master_second: float32 [1800, 1800], P(None, 'mdl')
- bfloat_second: bfloat16 [1800, 1800], P(None, 'mdl')
- momentum_final: float32 [1800, 32], P('mdl')
- variance_final: float32 [1800, 32], P('mdl')
- master_final: float32 [1800, 32], P('mdl')
- bfloat_final: bfloat16 [1800, 32], P('mdl')
- momentum_norm: float32 [4, 1800], P(None, 'mdl')
- variance_norm: float32 [4, 1800], P(None, 'mdl')
- master_norm: float32 [4, 1800], P(None, 'mdl')
- momentum_bias: float32 [32], replicated
- variance_bias: float32 [32], replicated
- master_bias: float32 [32], replicated
Inputs may be any that keep to these rules, and one draw needn't show every extreme that they name: `request_ids`: entries of row s * 8 + j lie in owner j's range j * 4096 to (j + 1) * 4096 - 1; the live ones (the first request_counts of the row) are distinct; the others are padding. `request_counts`: some owner receives exactly 1024 live ids from every device. `token_slots`: each token points at a live slot of its own device, and every live slot of a device is pointed at by one or more of its tokens.
All inputs are finite; a program needn't handle non-finite values.
Results may differ from a plain program's by a relative error of at most 0.003.
The roundings to bfloat16 on the way count: a program that leaves them out, or rounds other values in their place, can miss the bound.
Values may be sent and summed in bfloat16 or wider, within the bound.
A program may use at most 256 MiB of HBM per device.

v0:
```python
import jax
import jax.numpy as jnp
from jax import lax
from jax.sharding import PartitionSpec as P

STEP = 10


beta_one = 0.9
beta_two = 0.999
adam_epsilon = 1e-08
norm_epsilon = 1e-05
penalty_weight = 0.25
decay_matrix = 0.01
rate_matrix = 0.05
rate_norm = 0.5
rate_bias = 0.02


def mish(inputs):
    return inputs * jnp.tanh(jax.nn.softplus(inputs))


def mish_grad(inputs, upstream):
    _, pullback = jax.vjp(mish, inputs)
    return pullback(upstream)[0]


def contract(left, right, left_dim, right_dim):
    return lax.dot_general(
        left, right, (((left_dim,), (right_dim,)), ((), ())), preferred_element_type=jnp.float32
    )


def norm_back(upstream, unit_rows, gain_row, scale_row, live_mask, gain_sum, shift_sum, live_count):
    return scale_row * (
        gain_row * upstream
        - live_mask[:, None] * gain_row * (shift_sum + unit_rows * gain_sum) / live_count
    )


def adam(weight, moment, square, gradient, step_rate, shrink):
    momentum = beta_one * moment + (1.0 - beta_one) * gradient
    variance = beta_two * square + (1.0 - beta_two) * gradient * gradient
    moment_hat = momentum / (1.0 - beta_one**STEP)
    square_hat = variance / (1.0 - beta_two**STEP)
    master = weight - step_rate * (
        moment_hat / (jnp.sqrt(square_hat) + adam_epsilon) + shrink * weight
    )
    return (momentum, variance, master)


def body(
    hash_codes,
    request_ids,
    request_counts,
    token_slots,
    cotangent,
    weight_first,
    weight_second,
    weight_final,
    norm_params,
    bias_final,
    moment_first,
    square_first,
    moment_second,
    square_second,
    moment_final,
    square_final,
    moment_norm,
    square_norm,
    moment_bias,
    square_bias,
):
    owners = lax.axis_size("ids")
    owner_index = lax.axis_index("ids")
    range_rows = hash_codes.shape[0]
    slots_per = request_ids.shape[1]
    out_width = weight_final.shape[1]
    first_low = lax.all_gather(weight_first.astype(jnp.bfloat16), "ids", axis=0, tiled=True)
    second_low = weight_second.astype(jnp.bfloat16)
    final_low = weight_final.astype(jnp.bfloat16)
    received, arrived_counts = (
        lax.all_to_all(request_ids, "ids", split_axis=0, concat_axis=0, tiled=True),
        lax.all_to_all(request_counts, "ids", split_axis=0, concat_axis=0, tiled=True),
    )
    live_slot = (jnp.arange(slots_per)[None, :] < arrived_counts[:, None]).astype(jnp.float32)
    local_rows = (received - owner_index * range_rows).reshape(-1)
    hit_count = jax.ops.segment_sum(live_slot.reshape(-1), local_rows, num_segments=range_rows)
    live_mask = jnp.minimum(hit_count, 1.0)
    encoded = ((hash_codes.astype(jnp.float32) + 0.5) / 512.0 - 1.0).astype(jnp.bfloat16)
    features = lax.all_gather(encoded, "mdl", axis=1, tiled=True)
    linear_one = jnp.dot(features, first_low, preferred_element_type=jnp.float32)
    active_one = mish(linear_one)
    weighted_one = live_mask[:, None] * active_one
    sum_one, square_one, live_count = lax.psum(
        (jnp.sum(weighted_one, 0), jnp.sum(weighted_one * active_one, 0), jnp.sum(live_mask)), "ids"
    )
    mean_one = sum_one / live_count
    scale_one = lax.rsqrt(square_one / live_count - mean_one * mean_one + norm_epsilon)
    unit_one = (active_one - mean_one) * scale_one
    normed_one = (norm_params[0] * unit_one + norm_params[1]).astype(jnp.bfloat16)
    hidden_full = lax.all_gather(normed_one, "mdl", axis=1, tiled=True)
    linear_two = jnp.dot(hidden_full, second_low, preferred_element_type=jnp.float32)
    active_two = mish(linear_two)
    weighted_two = live_mask[:, None] * active_two
    sum_two, square_two = lax.psum(
        (jnp.sum(weighted_two, 0), jnp.sum(weighted_two * active_two, 0)), "ids"
    )
    mean_two = sum_two / live_count
    scale_two = lax.rsqrt(square_two / live_count - mean_two * mean_two + norm_epsilon)
    unit_two = (active_two - mean_two) * scale_two
    normed_two = (norm_params[2] * unit_two + norm_params[3]).astype(jnp.bfloat16)
    partial_embed = jnp.dot(normed_two, final_low, preferred_element_type=jnp.float32)
    embedding = lax.psum(partial_embed, "mdl") + bias_final
    embed_low = embedding.astype(jnp.bfloat16)
    replies = jnp.take(embed_low, local_rows, axis=0).reshape(owners, slots_per * out_width)
    returned = lax.all_to_all(replies, "ids", split_axis=0, concat_axis=0, tiled=True).reshape(
        owners * slots_per, out_width
    )
    token_embed = jnp.take(returned, token_slots, axis=0)
    token_total = token_slots.shape[0] * owners
    slot_grad = jax.ops.segment_sum(
        cotangent.astype(jnp.float32) / token_total, token_slots, num_segments=owners * slots_per
    )
    arrived = lax.all_to_all(
        slot_grad.reshape(owners, slots_per * out_width),
        "ids",
        split_axis=0,
        concat_axis=0,
        tiled=True,
    )
    row_grad = jax.ops.segment_sum(
        arrived.reshape(-1, out_width), local_rows, num_segments=range_rows
    )
    grad_embed = (
        row_grad + 2.0 * penalty_weight / live_count * live_mask[:, None] * embedding
    ).astype(jnp.bfloat16)
    local_final = contract(normed_two, grad_embed, 0, 0)
    local_bias = jnp.sum(grad_embed.astype(jnp.float32), 0)
    incoming_two = contract(grad_embed, final_low, 1, 1)
    gain_two, shift_two = lax.psum(
        (jnp.sum(incoming_two * unit_two, 0), jnp.sum(incoming_two, 0)), "ids"
    )
    outgoing_two = norm_back(
        incoming_two,
        unit_two,
        norm_params[2],
        scale_two,
        live_mask,
        gain_two,
        shift_two,
        live_count,
    )
    grad_linear_two = mish_grad(linear_two, outgoing_two).astype(jnp.bfloat16)
    local_second = contract(hidden_full, grad_linear_two, 0, 0)
    incoming_one = lax.psum_scatter(
        contract(second_low, grad_linear_two, 1, 1), "mdl", scatter_dimension=0, tiled=True
    ).T
    gain_one, shift_one, grad_second, grad_final, grad_bias = lax.psum(
        (
            jnp.sum(incoming_one * unit_one, 0),
            jnp.sum(incoming_one, 0),
            local_second,
            local_final,
            local_bias,
        ),
        "ids",
    )
    outgoing_one = norm_back(
        incoming_one,
        unit_one,
        norm_params[0],
        scale_one,
        live_mask,
        gain_one,
        shift_one,
        live_count,
    )
    grad_linear_one = mish_grad(linear_one, outgoing_one).astype(jnp.bfloat16)
    local_first = contract(features, grad_linear_one, 0, 0)
    grad_first = lax.psum_scatter(local_first, "ids", scatter_dimension=0, tiled=True)
    grad_norm = jnp.stack([gain_one, shift_one, gain_two, shift_two])
    momentum_first, variance_first, master_first = adam(
        weight_first, moment_first, square_first, grad_first, rate_matrix, decay_matrix
    )
    momentum_second, variance_second, master_second = adam(
        weight_second, moment_second, square_second, grad_second, rate_matrix, decay_matrix
    )
    momentum_final, variance_final, master_final = adam(
        weight_final, moment_final, square_final, grad_final, rate_matrix, decay_matrix
    )
    momentum_norm, variance_norm, master_norm = adam(
        norm_params, moment_norm, square_norm, grad_norm, rate_norm, 0.0
    )
    momentum_bias, variance_bias, master_bias = adam(
        bias_final, moment_bias, square_bias, grad_bias, rate_bias, 0.0
    )
    return (
        token_embed,
        momentum_first,
        variance_first,
        master_first,
        master_first.astype(jnp.bfloat16),
        momentum_second,
        variance_second,
        master_second,
        master_second.astype(jnp.bfloat16),
        momentum_final,
        variance_final,
        master_final,
        master_final.astype(jnp.bfloat16),
        momentum_norm,
        variance_norm,
        master_norm,
        momentum_bias,
        variance_bias,
        master_bias,
    )


def solution(mesh):
    return jax.shard_map(
        body,
        mesh=mesh,
        in_specs=(
            P("ids", "mdl"),
            P("ids", None),
            P("ids"),
            P("ids"),
            P("ids", None),
            P("ids", "mdl"),
            P(None, "mdl"),
            P("mdl", None),
            P(None, "mdl"),
            P(),
            P("ids", "mdl"),
            P("ids", "mdl"),
            P(None, "mdl"),
            P(None, "mdl"),
            P("mdl", None),
            P("mdl", None),
            P(None, "mdl"),
            P(None, "mdl"),
            P(),
            P(),
        ),
        out_specs=(
            P("ids", None),
            P("ids", "mdl"),
            P("ids", "mdl"),
            P("ids", "mdl"),
            P("ids", "mdl"),
            P(None, "mdl"),
            P(None, "mdl"),
            P(None, "mdl"),
            P(None, "mdl"),
            P("mdl", None),
            P("mdl", None),
            P("mdl", None),
            P("mdl", None),
            P(None, "mdl"),
            P(None, "mdl"),
            P(None, "mdl"),
            P(),
            P(),
            P(),
        ),
        check_vma=False,
    )
```

profile of v0, /device:TPU:0, one launch (start us, length us, event | category | flops | bytes accessed | tf_op | source)
XLA Modules:
  0.0 1157.3 jit_solution(2867318164478680946)
XLA Ops:
  7.3 4.2 add_convert_fusion.2
  12.2 7.3 all-to-all-start.1
  20.2 30.5 %all_gather.10 = bf16[1024,450]{0,1:T(8,128)(2,1)S(1)} all-gather(bf16[128,450]{0,1:T(8,128)(2,1)S(1)} %convert_element_type.57), channel_id=1, replica_groups=mesh['ids'=8,'mdl'=4] {'ids'}, dimensions={0}, use_global_device_ids=true | all-gather | bytes 1036800 | tf_op jit(solution)/shard_map/all_gather | solution.py:80
  50.7 3.3 all-to-all-start
  54.4 6.2 all-to-all-done
  60.6 43.2 %scatter_custom_fusion = f32[4096]{0:T(1024)S(1)} fusion(s32[8192]{0:T(1024)S(1)} %bitcast.51, f32[8192]{0:T(1024)S(1)} %bitcast.57, f32[]{:T(128)} %constant.41.clone.1), kind=kCustom, calls=%fused_computation.93 | custom fusion | flops 8192 | bytes 16388 | tf_op jit(solution)/shard_map/scatter-add | solution.py:89
  104.5 11.6 multiply_reduce_fusion.1
  116.0 19.1 %all-reduce.4 = (f32[450]{0:T(512)S(1)}, f32[]{:T(128)}, f32[450]{0:T(512)S(1)}) all-reduce(f32[450]{0:T(512)S(1)} %get-tuple-element.106, f32[]{:T(128)} %get-tuple-element.140, f32[450]{0:T(512)S(1)} %get-tuple-element.105), channel_id=1, replica_groups=mesh['ids'=8,'mdl'=4] {'ids'}, use_global_device_ids=true, to_apply=%region_6.7 | all-reduce | flops 901 | bytes 7208 | tf_op jit(solution)/shard_map/psum | solution.py:96
  135.9 9.9 fusion.15
  145.9 2.7 copy.55
  148.6 46.6 %scatter_custom_fusion.1 = f32[8192,32]{1,0:T(8,128)} fusion(s32[8192]{0:T(1024)S(1)} %copy-done.11, f32[8192,32]{1,0:T(8,128)} %copy.55, f32[]{:T(128)} %constant.41.clone.1), kind=kCustom, calls=%fused_computation.53 | custom fusion | flops 262144 | bytes 1049088 | tf_op jit(solution)/shard_map/scatter-add | solution.py:123
  195.2 4.8 all_to_all.29
  200.0 3.6 all-to-all-start.3
  203.8 35.7 %all-gather.6.cloned.1.call-done = bf16[4,450,4096]{2,1,0:T(8,128)(2,1)} async-done(((bf16[1,450,4096]{2,1,0:T(8,128)(2,1)}), bf16[4,450,4096]{2,1,0:T(8,128)(2,1)}) %all-gather.6.cloned.1.call-update) | async-done | bytes 14745616 | tf_op jit(solution)/shard_map/all_gather | solution.py:103
  239.5 14.3 %reshape.186 = bf16[1800,4096]{1,0:T(8,128)(2,1)} reshape(bf16[4,450,4096]{2,1,0:T(8,128)(2,1)} %all-gather.6.cloned.1.call-done) | data formatting | bytes 29491200
  253.8 19.0 %multiply_reduce_fusion = (f32[450]{0:T(512)S(1)}, f32[450]{0:T(512)S(1)}, f32[4096,450]{0,1:T(8,128)}) fusion(f32[4096]{0:T(1024)S(1)} %get-tuple-element.141, bf16[1800,4096]{1,0:T(8,128)(2,1)} %reshape.186, f32[1800,450]{0,1:T(8,128)} %param.27), kind=kOutput, calls=%fused_computation.13 | convolution fusion | flops 6656604160 | bytes 25378384 | tf_op jit(solution)/shard_map/dot_general | solution.py:104
  272.8 21.7 %all-reduce.3 = (f32[450]{0:T(512)S(1)}, f32[450]{0:T(512)S(1)}) all-reduce(f32[450]{0:T(512)S(1)} %get-tuple-element.104, f32[450]{0:T(512)S(1)} %get-tuple-element.103), channel_id=1, replica_groups=mesh['ids'=8,'mdl'=4] {'ids'}, use_global_device_ids=true, to_apply=%region_10.11 | all-reduce | flops 900 | bytes 7200 | tf_op jit(solution)/shard_map/psum | solution.py:107
  295.1 8.6 add_convert_fusion
  303.8 1.9 copy-done
  307.3 2.5 reduce.3
  309.8 3.4 reshape.177
  313.9 23.2 %all-reduce.9.cloned.1.call-done = f32[4096,32]{0,1:T(8,128)} async-done(((f32[4096,32]{0,1:T(8,128)}), f32[4096,32]{0,1:T(8,128)}) %all-reduce.9.cloned.1.call-update) | async-done | bytes 524304 | tf_op jit(solution)/shard_map/psum | solution.py:115
  338.9 45.5 %scatter_fusion = f32[4096,32]{1,0:T(8,128)S(1)} fusion(f32[4096,32]{1,0:T(8,128)S(1)} %copy.57, s32[8192]{0:T(1024)S(1)} %bitcast.52, f32[8192,32]{1,0:T(8,128)} %reshape.177), kind=kCustom, calls=%fused_computation.4 | custom fusion | flops 262144 | bytes 3178496 | tf_op jit(solution)/shard_map/scatter-add | solution.py:133
  384.4 10.0 fusion.43
  394.4 21.3 %all-reduce.2 = (f32[450]{0:T(512)S(1)}, f32[450]{0:T(512)S(1)}) all-reduce(f32[450]{0:T(512)S(1)} %get-tuple-element.108, f32[450]{0:T(512)S(1)} %get-tuple-element.107), channel_id=1, replica_groups=mesh['ids'=8,'mdl'=4] {'ids'}, use_global_device_ids=true, to_apply=%region_17.18 | all-reduce | flops 900 | bytes 7200 | tf_op jit(solution)/shard_map/psum | solution.py:142
  415.8 14.4 %fusion.6 = bf16[4096,450]{0,1:T(8,128)(2,1)S(1)} fusion(f32[4096,450]{0,1:T(8,128)} %get-tuple-element.151, f32[4096,450]{0,1:T(8,128)} %get-tuple-element.152, f32[]{:T(128)} %get-tuple-element.118, f32[450]{0:T(512)S(1)} %get-tuple-element.113, f32[450]{0:T(512)S(1)} %get-tuple-element.114, f32[450]{0:T(512)S(1)} %get-tuple-element.147, ...), kind=kLoop, calls=%fused_computation.22 | loop fusion | flops 57139200 | bytes 18457388 | tf_op jit(solution)/shard_map/convert_element_type | solution.py:155
  430.2 1.9 copy-done.2
  432.1 13.6 %convolution_bitcast_fusion = f32[1800,4096]{1,0:T(8,128)} fusion(bf16[4096,450]{0,1:T(8,128)(2,1)S(1)} %fusion.6, f32[1800,450]{0,1:T(8,128)S(1)} %copy-done.3), kind=kOutput, calls=%fused_computation.11 | convolution fusion | flops 6636329984 | bytes 36417600 | tf_op jit(solution)/shard_map/dot_general | solution.py:30
  448.2 2.2 broadcast_in_dim.61
  450.4 3.0 broadcast_in_dim.62
  453.9 29.6 %gather_fusion = bf16[8192,32]{1,0:T(8,128)(2,1)} fusion(bf16[4096,32]{1,0:T(8,128)(2,1)S(1)} %copy.53, s32[8192]{0:T(1024)S(1)} %broadcast_clamp_fusion), kind=kCustom, calls=%fused_computation | custom fusion | bytes 1081344 | tf_op jit(solution)/shard_map/jit(_take)/gather | solution.py:117
  483.6 3.8 gather.11
  490.2 3.5 all-to-all-start.2
  493.8 14.0 %fusion.53 = f32[1800,450]{0,1:T(8,128)} fusion(bf16[1800,4096]{1,0:T(8,128)(2,1)} %reshape.186, bf16[4096,450]{0,1:T(8,128)(2,1)} %copy-done.2), kind=kOutput, calls=%fused_computation.118 | convolution fusion | flops 6635520000 | bytes 21672000 | tf_op jit(solution)/shard_map/dot_general | solution.py:30
  508.4 3.2 fusion.37
  512.4 3.2 reduce.2
  517.2 29.5 %gather_fusion.1 = bf16[8192,32]{1,0:T(8,128)(2,1)} fusion(bf16[8192,32]{1,0:T(8,128)(2,1)S(1)} %reshape.138, s32[8192]{0:T(1024)S(1)} %fusion.26), kind=kCustom, calls=%fused_computation.1 | custom fusion | bytes 1081344 | tf_op jit(solution)/shard_map/jit(_take)/gather | solution.py:121
  546.7 388.2 %all-reduce.13.cloned.1.call-done = f32[1800,4096]{1,0:T(8,128)} async-done(((f32[1800,4096]{1,0:T(8,128)}), f32[1800,4096]{1,0:T(8,128)}) %all-reduce.13.cloned.1.call-update) | async-done | bytes 29491216
  934.9 4.0 dynamic-slice_reduce_fusion
  938.9 9.2 fusion.14
  948.2 41.4 %all-reduce.1 = (f32[450]{0:T(512)S(1)}, f32[450]{0:T(512)S(1)}, f32[450,32]{0,1:T(8,128)S(1)}, f32[32]{0:T(128)S(1)}) all-reduce(f32[450]{0:T(512)S(1)} %fusion.14, f32[450]{0:T(512)S(1)} %dynamic-slice_reduce_fusion, f32[450,32]{0,1:T(8,128)S(1)} %fusion.37, f32[32]{0:T(128)S(1)} %convert_reduce_fusion), channel_id=1, replica_groups=mesh['ids'=8,'mdl'=4] {'ids'}, use_global_device_ids=true, to_apply=%region_22.24 | all-reduce | flops 15332 | bytes 122656 | tf_op jit(solution)/shard_map/psum | solution.py:160
  989.6 20.5 %fusion.16 = f32[1024,450]{0,1:T(8,128)} fusion(bf16[4096,1024]{1,0:T(8,128)(2,1)} %all-gather.4.cloned.1.call-done, f32[4096,450]{0,1:T(8,128)} %get-tuple-element.150, f32[1800,4096]{1,0:T(8,128)} %all-reduce.13.cloned.1.call-done, u32[]{:T(128)S(6)} %multiply.13, f32[450]{0:T(512)S(1)} %get-tuple-element.109, f32[450]{0:T(512)S(1)} %get-tuple-element.110, ...), kind=kOutput, calls=%fused_computation.48 | convolution fusion | flops 3832012800 | bytes 25199916 | tf_op jit(solution)/shard_map/dot_general | solution.py:30
  1010.2 5.0 broadcast_select_fusion
  1015.2 2.6 copy.58
  1018.0 61.7 %all-reduce.11.cloned.1.call-done = f32[1800,450]{0,1:T(8,128)} async-done(((f32[1800,450]{0,1:T(8,128)}), f32[1800,450]{0,1:T(8,128)}) %all-reduce.11.cloned.1.call-update) | async-done | bytes 3240016 | tf_op jit(solution)/shard_map/psum | solution.py:160
  1079.7 9.0 fusion.48
  1090.6 57.7 %reduce-scatter.2.cloned.1.call-done = f32[128,450]{0,1:T(8,128)} async-done(((f32[1024,450]{0,1:T(8,128)}), f32[128,450]{0,1:T(8,128)}) %reduce-scatter.2.cloned.1.call-update) | async-done | bytes 230416 | tf_op jit(solution)/shard_map/reduce_scatter | solution.py:182
  1148.2 1.9 fusion.50
  (119 shorter events, 17.7 us)
Async XLA Ops:
  7.2 4.3 copy-start.32
  7.2 12.3 %copy-start.17 = (s32[8,1024]{1,0:T(8,128)S(1)}, s32[8,1024]{1,0:T(8,128)}, u32[]{:S(2)}) copy-start(s32[8,1024]{1,0:T(8,128)} %param.22) | copy-start | bytes 98308
  7.2 12.9 %copy-start.5 = (f32[128,450]{0,1:T(8,128)S(1)}, f32[128,450]{0,1:T(8,128)}, u32[]{:S(2)}) copy-start(f32[128,450]{0,1:T(8,128)} %param.26) | copy-start | bytes 691204
  7.2 12.9 %copy-start.15 = (f32[4,450]{1,0:T(4,128)S(1)}, f32[4,450]{1,0:T(4,128)}, u32[]{:S(2)}) copy-start(f32[4,450]{1,0:T(4,128)} %param.29) | copy-start | bytes 21604
  7.2 97.2 %all-gather.4.cloned.1.call-start = ((), (), s32[]{:S(2)}) async-start(), calls=%async_computation.5 | async-start | bytes 10485760 | tf_op jit(solution)/shard_map/all_gather | solution.py:92
  12.2 38.5 %all-to-all-start.1 = ((s32[8,1,1]{2,1,0:T(1,128)}), s32[8,1,1]{2,1,0:T(1,128)S(1)}, u32[]{:S(2)}, u32[]{:S(2)}) async-start(s32[8,1,1]{2,1,0:T(1,128)} %copy.52), calls=%async_computation.1 | async-start | bytes 8192 | tf_op jit(solution)/shard_map/all_to_all | solution.py:85
  20.1 115.7 %copy-start.26 = (f32[1,450]{1,0:T(1,128)}, f32[1,450]{1,0:T(1,128)S(1)}, u32[]{:S(2)}) copy-start(f32[1,450]{1,0:T(1,128)S(1)} %get-tuple-element.144) | copy-start | bytes 5404
  50.7 10.0 all-to-all-start
  54.0 185.5 %all-gather.6.cloned.1.call-start = ((), (), s32[]{:S(2)}) async-start(), calls=%async_computation.9 | async-start | bytes 18677760 | tf_op jit(solution)/shard_map/all_gather | solution.py:103
  135.8 10.0 copy-start.18
  135.8 10.0 copy-start.20
  135.9 10.0 copy-start.7
  145.8 2.8 copy-start.11
  200.0 107.3 %all-to-all-start.3 = ((f32[8,1,32768]{2,1,0:T(1,128)}), f32[8,1,32768]{2,1,0:T(1,128)S(1)}, u32[]{:S(2)}, u32[]{:S(2)}) async-start(f32[8,1,32768]{2,1,0:T(1,128)} %all_to_all.29), calls=%async_computation.3 | async-start | bytes 2097152 | tf_op jit(solution)/shard_map/all_to_all | solution.py:126
  203.6 133.5 %all-reduce.9.cloned.1.call-start = ((), (), s32[]{:S(2)}) async-start(), calls=%async_computation.6 | async-start | bytes 1048576 | tf_op jit(solution)/shard_map/psum | solution.py:115
  272.8 32.9 %copy-start.8 = (f32[450,32]{0,1:T(8,128)S(1)}, f32[450,32]{0,1:T(8,128)}, u32[]{:S(2)}) copy-start(f32[450,32]{0,1:T(8,128)} %param.28) | copy-start | bytes 172804
  303.8 1.9 copy-start
  305.7 31.5 %copy-start.30 = (f32[32]{0:T(128)S(1)}, f32[32]{0:T(128)}, u32[]{:S(2)}) copy-start(f32[32]{0:T(128)} %param.30) | copy-start | bytes 388
  307.2 627.7 %all-reduce.13.cloned.1.call-start = ((), (), s32[]{:S(2)}) async-start(), calls=%async_computation.10 | async-start | bytes 58982400
  415.8 14.4 %copy-start.22 = (f32[450]{0:T(512)}, f32[450]{0:T(512)S(1)}, u32[]{:S(2)}) copy-start(f32[450]{0:T(512)S(1)} %get-tuple-element.113) | copy-start | bytes 5404
  415.8 14.4 %copy-start.24 = (f32[450]{0:T(512)}, f32[450]{0:T(512)S(1)}, u32[]{:S(2)}) copy-start(f32[450]{0:T(512)S(1)} %get-tuple-element.114) | copy-start | bytes 5404
  415.8 16.3 %copy-start.3 = (f32[1800,450]{0,1:T(8,128)S(1)}, f32[1800,450]{0,1:T(8,128)}, u32[]{:S(2)}) copy-start(f32[1800,450]{0,1:T(8,128)} %param.27) | copy-start | bytes 9720004
  430.2 1.9 copy-start.2
  445.7 0.7 copy-start.35
  453.9 33.5 %copy-start.4 = (pred[8,1,32768]{2,0,1:T(8,128)(4,1)S(1)}, pred[8,1,32768]{2,0,1:T(8,128)(4,1)}, u32[]{:S(2)}) copy-start(pred[8,1,32768]{2,0,1:T(8,128)(4,1)} %broadcast_in_dim.62) | copy-start | bytes 786436
  490.2 21.4 %all-to-all-start.2 = ((bf16[8,2,16384]{2,1,0:T(2,128)(2,1)}), bf16[8,2,16384]{2,1,0:T(2,128)(2,1)S(1)}, u32[]{:S(2)}, u32[]{:S(2)}) async-start(bf16[8,2,16384]{2,1,0:T(2,128)(2,1)} %reshape.195), calls=%async_computation.2 | async-start | bytes 1048576 | tf_op jit(solution)/shard_map/all_to_all | solution.py:118
  493.7 586.0 %all-reduce.11.cloned.1.call-start = ((), (), s32[]{:S(2)}) async-start(), calls=%async_computation.8 | async-start | bytes 7004160 | tf_op jit(solution)/shard_map/psum | solution.py:160
  507.8 640.4 %reduce-scatter.2.cloned.1.call-start = ((), (), s32[]{:S(2)}) async-start(), calls=%async_computation.7 | async-start | bytes 2101248 | tf_op jit(solution)/shard_map/reduce_scatter | solution.py:182
  546.7 392.2 %copy-start.19 = (f32[450]{0:T(512)S(1)}, f32[450]{0:T(512)}, u32[]{:S(2)}) copy-start(f32[450]{0:T(512)} %copy-done.18) | copy-start | bytes 5404
  546.7 392.2 %copy-start.21 = (f32[450]{0:T(512)S(1)}, f32[450]{0:T(512)}, u32[]{:S(2)}) copy-start(f32[450]{0:T(512)} %copy-done.20) | copy-start | bytes 5404
  938.9 50.6 %copy-start.27 = (f32[1,450]{1,0:T(1,128)S(1)}, f32[1,450]{1,0:T(1,128)}, u32[]{:S(2)}) copy-start(f32[1,450]{1,0:T(1,128)} %copy-done.26) | copy-start | bytes 5404
  989.6 20.6 %copy-start.1 = (bf16[8192,32]{1,0:T(8,128)(2,1)S(1)}, bf16[8192,32]{1,0:T(8,128)(2,1)}, u32[]{:S(2)}) copy-start(bf16[8192,32]{1,0:T(8,128)(2,1)} %gather_fusion.1) | copy-start | bytes 1572868
  989.6 20.6 %copy-start.14 = (pred[8192]{0:T(1024)(128)(4,1)S(1)}, pred[8192]{0:T(1024)(128)(4,1)}, u32[]{:S(2)}) copy-start(pred[8192]{0:T(1024)(128)(4,1)} %compare_and_fusion.1) | copy-start | bytes 24580
  1017.8 70.8 %copy-start.31 = (f32[32]{0:T(128)S(1)}, f32[32]{0:T(128)}, u32[]{:S(2)}) copy-start(f32[32]{0:T(128)} %param.30) | copy-start | bytes 388
  1017.8 70.8 %copy-start.33 = (f32[32]{0:T(128)S(1)}, f32[32]{0:T(128)}, u32[]{:S(2)}) copy-start(f32[32]{0:T(128)} %param.40) | copy-start | bytes 388
  1017.8 70.8 %copy-start.34 = (f32[32]{0:T(128)S(1)}, f32[32]{0:T(128)}, u32[]{:S(2)}) copy-start(f32[32]{0:T(128)} %param.39) | copy-start | bytes 388
  1017.8 71.4 %copy-start.16 = (f32[4,450]{1,0:T(4,128)S(1)}, f32[4,450]{1,0:T(4,128)}, u32[]{:S(2)}) copy-start(f32[4,450]{1,0:T(4,128)} %param.29) | copy-start | bytes 21604
  1017.9 71.3 %copy-start.23 = (f32[450]{0:T(512)S(1)}, f32[450]{0:T(512)}, u32[]{:S(2)}) copy-start(f32[450]{0:T(512)} %copy-done.22) | copy-start | bytes 5404
  1017.9 71.3 %copy-start.25 = (f32[450]{0:T(512)S(1)}, f32[450]{0:T(512)}, u32[]{:S(2)}) copy-start(f32[450]{0:T(512)} %copy-done.24) | copy-start | bytes 5404
  1017.9 71.3 %copy-start.28 = (f32[4,450]{1,0:T(4,128)S(1)}, f32[4,450]{1,0:T(4,128)}, u32[]{:S(2)}) copy-start(f32[4,450]{1,0:T(4,128)} %param.38) | copy-start | bytes 21604
  1017.9 71.3 %copy-start.29 = (f32[4,450]{1,0:T(4,128)S(1)}, f32[4,450]{1,0:T(4,128)}, u32[]{:S(2)}) copy-start(f32[4,450]{1,0:T(4,128)} %param.37) | copy-start | bytes 21604
  1017.9 72.0 %copy-start.12 = (f32[450,32]{0,1:T(8,128)S(1)}, f32[450,32]{0,1:T(8,128)}, u32[]{:S(2)}) copy-start(f32[450,32]{0,1:T(8,128)} %param.36) | copy-start | bytes 172804
  1017.9 72.0 %copy-start.13 = (f32[450,32]{0,1:T(8,128)S(1)}, f32[450,32]{0,1:T(8,128)}, u32[]{:S(2)}) copy-start(f32[450,32]{0,1:T(8,128)} %param.35) | copy-start | bytes 172804
  1017.9 130.3 %copy-start.6 = (f32[128,450]{0,1:T(8,128)S(1)}, f32[128,450]{0,1:T(8,128)}, u32[]{:S(2)}) copy-start(f32[128,450]{0,1:T(8,128)} %param.26) | copy-start | bytes 691204
  1017.9 130.3 %copy-start.9 = (f32[128,450]{0,1:T(8,128)S(1)}, f32[128,450]{0,1:T(8,128)}, u32[]{:S(2)}) copy-start(f32[128,450]{0,1:T(8,128)} %param.32) | copy-start | bytes 691204
  1017.9 130.3 %copy-start.10 = (f32[128,450]{0,1:T(8,128)S(1)}, f32[128,450]{0,1:T(8,128)}, u32[]{:S(2)}) copy-start(f32[128,450]{0,1:T(8,128)} %param.31) | copy-start | bytes 691204
Sparse Core Ops, SparseCore 0:
  11.6 62.0 all-gather.3
  145.9 93.5 all-gather.5
  307.4 29.7 all-reduce.8
  445.8 489.0 all-reduce.12
  939.0 140.6 all-reduce.10
  1083.0 65.1 reduce-scatter.1
where the time goes:
time: 1160 us
  waiting for transfers between devices  573 us (49%)
  other arithmetic  215 us (19%)
  blocking collectives  134 us (12%)
  local copies, waits for them, and re-layouts  108 us (9%)
  matrix products  93.4 us (8%)
  starting transfers between devices  18.1 us (2%)
  between operations  16.4 us (1%)
    unnamed x7, waiting for transfers between devices  388 us
    psum x1, waiting for transfers between devices, body(): lax.psum((jnp.sum(incoming_one * unit_one, 0), jnp.sum(incoming_one, 0),...  61.7 us
    dot_general x5, matrix products, contract(): lax.dot_general(left, right, (((left_dim,), (right_dim,)), ((), ())), pre...  61.4 us
    reduce_scatter x1, waiting for transfers between devices, body(): lax.psum_scatter(local_first, 'ids', scatter_dimension=0, tiled=True)  57.7 us
    scatter-add x1, other arithmetic, body(): jax.ops.segment_sum(cotangent.astype(jnp.float32) / token_total, token_sl...  46.6 us
    scatter-add x1, other arithmetic, body(): jax.ops.segment_sum(arrived.reshape(-1, out_width), local_rows, num_segme...  45.5 us
    scatter-add x1, other arithmetic, body(): jax.ops.segment_sum(live_slot.reshape(-1), local_rows, num_segments=range...  43.2 us
    psum x1, blocking collectives, body(): lax.psum((jnp.sum(incoming_one * unit_one, 0), jnp.sum(incoming_one, 0),...  41.4 us
  transfers between devices with their start and end apart: 10, of which 6 were waited for; matrix products, arithmetic and copies ran while one was open for 25% of the time, Pallas kernels for 0%

commit v1 on v0

v1 whole, which is shorter than its diff:
```python
import jax
import jax.numpy as jnp
from jax import lax
from jax.sharding import PartitionSpec as P

STEP = 10


beta_one = 0.9
beta_two = 0.999
adam_epsilon = 1e-08
norm_epsilon = 1e-05
penalty_weight = 0.25
decay_matrix = 0.01
rate_matrix = 0.05
rate_norm = 0.5
rate_bias = 0.02
LANES = 128


def mish_parts(inputs):
    grown = jnp.exp(jnp.minimum(inputs, 20.0))
    above = grown * (grown + 2.0)
    inverse = 1.0 / (above + 2.0)
    return grown, above * inverse, inverse


def mish(inputs):
    return inputs * mish_parts(inputs)[1]


def mish_slope(inputs):
    grown, gate, inverse = mish_parts(inputs)
    return gate + 4.0 * jnp.minimum(inputs, 20.0) * (grown * inverse) * ((1.0 + grown) * inverse)


def contract(left, right, left_dim, right_dim):
    return lax.dot_general(
        left, right, (((left_dim,), (right_dim,)), ((), ())), preferred_element_type=jnp.float32
    )


def norm_back(upstream, unit_rows, gain_row, scale_row, live_mask, gain_sum, shift_sum, live_count):
    return scale_row * (
        gain_row * upstream
        - live_mask[:, None] * gain_row * (shift_sum + unit_rows * gain_sum) / live_count
    )


def adam(weight, moment, square, gradient, step_rate, shrink):
    momentum = beta_one * moment + (1.0 - beta_one) * gradient
    variance = beta_two * square + (1.0 - beta_two) * gradient * gradient
    moment_hat = momentum / (1.0 - beta_one**STEP)
    square_hat = variance / (1.0 - beta_two**STEP)
    master = weight - step_rate * (
        moment_hat / (jnp.sqrt(square_hat) + adam_epsilon) + shrink * weight
    )
    return (momentum, variance, master)


def split_two(values):
    high = values.astype(jnp.bfloat16)
    low = (values - high.astype(jnp.float32)).astype(jnp.bfloat16)
    return high, low


def one_hot(index, length, first):
    rows = lax.broadcasted_iota(jnp.int32, (length, index.shape[0]), 0) + first
    return (rows == index[None, :]).astype(jnp.bfloat16)


def body(
    hash_codes,
    request_ids,
    request_counts,
    token_slots,
    cotangent,
    weight_first,
    weight_second,
    weight_final,
    norm_params,
    bias_final,
    moment_first,
    square_first,
    moment_second,
    square_second,
    moment_final,
    square_final,
    moment_norm,
    square_norm,
    moment_bias,
    square_bias,
):
    owners = lax.axis_size("ids")
    parts = lax.axis_size("mdl")
    part = lax.axis_index("mdl")
    both = ("ids", "mdl")
    range_rows = hash_codes.shape[0]
    rows = range_rows // parts
    slots_per = request_ids.shape[1]
    piece = slots_per // parts
    out_width = weight_final.shape[1]
    width = weight_first.shape[1]
    wide = width + (-width) % LANES
    hidden = wide * parts
    more = wide - width
    token_count = token_slots.shape[0]
    token_piece = token_count // parts
    token_total = token_count * owners

    first_part = jnp.pad(weight_first.astype(jnp.bfloat16), ((0, 0), (0, more)))
    first_low = lax.all_gather(first_part, "ids", axis=0, tiled=True)
    first_low = lax.all_gather(first_low, "mdl", axis=1, tiled=True)
    second_part = jnp.pad(
        weight_second.astype(jnp.bfloat16).reshape(parts, width, width),
        ((0, 0), (0, more), (0, more)),
    ).reshape(hidden, wide)
    second_low = lax.all_gather(second_part, "mdl", axis=1, tiled=True)
    final_part = jnp.pad(weight_final.astype(jnp.bfloat16), ((0, more), (0, 0)))
    final_low = lax.all_gather(final_part, "mdl", axis=0, tiled=True)
    norm_all = lax.all_gather(jnp.pad(norm_params, ((0, 0), (0, more))), "mdl", axis=1, tiled=True)

    encoded = ((hash_codes.astype(jnp.float32) + 0.5) / 512.0 - 1.0).astype(jnp.bfloat16)
    features = lax.all_to_all(encoded, "mdl", split_axis=0, concat_axis=1, tiled=True)

    owner_row = jnp.arange(owners, dtype=jnp.int32)[:, None]
    wanted = jnp.where(
        jnp.arange(slots_per, dtype=jnp.int32)[None, :] < request_counts[:, None],
        request_ids - owner_row * range_rows,
        range_rows,
    )
    received = lax.all_to_all(wanted, "ids", split_axis=0, concat_axis=0, tiled=True)

    slot_owner = token_slots // slots_per
    slot_place = token_slots % slots_per - part * piece
    slot_here = jnp.where(
        (slot_place >= 0) & (slot_place < piece), slot_owner * piece + slot_place, -1
    )
    slot_sum = jnp.dot(
        one_hot(slot_here, owners * piece, 0), cotangent, preferred_element_type=jnp.float32
    ) / token_total
    high, low = split_two(slot_sum)
    sent = jnp.concatenate([high, low], axis=1).reshape(owners, piece * 2 * out_width)
    arrived = lax.all_to_all(sent, "ids", split_axis=0, concat_axis=0, tiled=True)
    arrived = lax.all_gather(arrived.reshape(owners * piece, 2 * out_width), "mdl", axis=0, tiled=False)
    arrived = arrived.reshape(parts * owners * piece, 2 * out_width)
    slot_rows = received.reshape(owners, parts, piece).transpose(1, 0, 2)
    slot_rows = slot_rows.reshape(-1)
    marked = jnp.concatenate(
        [arrived, jnp.ones((arrived.shape[0], 2 * out_width), jnp.bfloat16)], axis=1
    )
    row_sums = jnp.dot(
        one_hot(slot_rows, rows, part * rows), marked, preferred_element_type=jnp.float32
    )
    row_grad = row_sums[:, :out_width] + row_sums[:, out_width : 2 * out_width]
    live_mask = jnp.minimum(row_sums[:, 2 * out_width], 1.0)

    linear_one = jnp.dot(features, first_low, preferred_element_type=jnp.float32)
    active_one = mish(linear_one)
    weighted_one = live_mask[:, None] * active_one
    sums_one = jnp.stack([jnp.sum(weighted_one, 0), jnp.sum(weighted_one * active_one, 0)])
    sums_one, live_count = lax.psum((sums_one, jnp.sum(live_mask)), both)
    mean_one = sums_one[0] / live_count
    scale_one = lax.rsqrt(sums_one[1] / live_count - mean_one * mean_one + norm_epsilon)
    unit_one = (active_one - mean_one) * scale_one
    normed_one = (norm_all[0] * unit_one + norm_all[1]).astype(jnp.bfloat16)
    linear_two = jnp.dot(normed_one, second_low, preferred_element_type=jnp.float32)
    active_two = mish(linear_two)
    weighted_two = live_mask[:, None] * active_two
    sums_two = lax.psum(
        jnp.stack([jnp.sum(weighted_two, 0), jnp.sum(weighted_two * active_two, 0)]), both
    )
    mean_two = sums_two[0] / live_count
    scale_two = lax.rsqrt(sums_two[1] / live_count - mean_two * mean_two + norm_epsilon)
    unit_two = (active_two - mean_two) * scale_two
    normed_two = (norm_all[2] * unit_two + norm_all[3]).astype(jnp.bfloat16)
    embedding = jnp.dot(normed_two, final_low, preferred_element_type=jnp.float32) + bias_final
    embed_low = embedding.astype(jnp.bfloat16)

    embed_range = lax.all_gather(embed_low, "mdl", axis=0, tiled=True)
    slots_mine = lax.dynamic_slice(received, (0, part * piece), (owners, piece)).reshape(-1)
    pick_rows = (
        slots_mine[:, None] == lax.broadcasted_iota(jnp.int32, (owners * piece, range_rows), 1)
    ).astype(jnp.bfloat16)
    replies = jnp.dot(pick_rows, embed_range, preferred_element_type=jnp.float32)
    replies = replies.astype(jnp.bfloat16).reshape(owners, piece * out_width)
    returned = lax.all_to_all(replies, "ids", split_axis=0, concat_axis=0, tiled=True)
    returned = lax.all_gather(returned.reshape(owners, piece, out_width), "mdl", axis=1, tiled=True)
    returned = returned.reshape(owners * slots_per, out_width)
    tokens_mine = lax.dynamic_slice(token_slots, (part * token_piece,), (token_piece,))
    pick_slots = (
        tokens_mine[:, None]
        == lax.broadcasted_iota(jnp.int32, (token_piece, owners * slots_per), 1)
    ).astype(jnp.bfloat16)
    token_part = jnp.dot(pick_slots, returned, preferred_element_type=jnp.float32)
    token_embed = lax.all_gather(token_part.astype(jnp.bfloat16), "mdl", axis=0, tiled=True)

    grad_embed = (
        row_grad + 2.0 * penalty_weight / live_count * live_mask[:, None] * embedding
    ).astype(jnp.bfloat16)
    incoming_two = contract(grad_embed, final_low, 1, 1)
    sums_two = lax.psum(
        jnp.stack([jnp.sum(incoming_two * unit_two, 0), jnp.sum(incoming_two, 0)]), both
    )
    local_final = contract(normed_two, grad_embed, 0, 0)
    local_bias = jnp.sum(grad_embed.astype(jnp.float32), 0)
    outgoing_two = norm_back(
        incoming_two, unit_two, norm_all[2], scale_two, live_mask, sums_two[0], sums_two[1], live_count
    )
    grad_linear_two = (mish_slope(linear_two) * outgoing_two).astype(jnp.bfloat16)
    local_second = jnp.stack(
        [
            contract(normed_one, grad_linear_two[:, wide * k : wide * (k + 1)], 0, 0)
            for k in range(parts)
        ]
    )
    grad_second = lax.psum_scatter(local_second, "mdl", scatter_dimension=0, tiled=False)
    grad_second = lax.psum(grad_second, "ids")
    grad_second = grad_second.reshape(parts, wide, wide)[:, :width, :width].reshape(-1, width)
    incoming_one = contract(grad_linear_two, second_low, 1, 1)
    sums_one, final_sum, grad_bias = lax.psum(
        (
            jnp.stack([jnp.sum(incoming_one * unit_one, 0), jnp.sum(incoming_one, 0)]),
            local_final,
            local_bias,
        ),
        both,
    )
    outgoing_one = norm_back(
        incoming_one, unit_one, norm_all[0], scale_one, live_mask, sums_one[0], sums_one[1], live_count
    )
    grad_linear_one = (mish_slope(linear_one) * outgoing_one).astype(jnp.bfloat16)
    local_first = jnp.stack(
        [
            contract(features, grad_linear_one[:, wide * k : wide * (k + 1)], 0, 0)
            for k in range(parts)
        ]
    )
    grad_first = lax.psum_scatter(local_first, "mdl", scatter_dimension=0, tiled=False)
    grad_first = lax.psum_scatter(grad_first, "ids", scatter_dimension=0, tiled=True)[:, :width]

    start = part * wide
    grad_final = lax.dynamic_slice(final_sum, (start, 0), (width, out_width))
    grad_norm = lax.dynamic_slice(
        jnp.concatenate([sums_one, sums_two]), (0, start), (4, width)
    )
    momentum_first, variance_first, master_first = adam(
        weight_first, moment_first, square_first, grad_first, rate_matrix, decay_matrix
    )
    momentum_second, variance_second, master_second = adam(
        weight_second, moment_second, square_second, grad_second, rate_matrix, decay_matrix
    )
    momentum_final, variance_final, master_final = adam(
        weight_final, moment_final, square_final, grad_final, rate_matrix, decay_matrix
    )
    momentum_norm, variance_norm, master_norm = adam(
        norm_params, moment_norm, square_norm, grad_norm, rate_norm, 0.0
    )
    momentum_bias, variance_bias, master_bias = adam(
        bias_final, moment_bias, square_bias, grad_bias, rate_bias, 0.0
    )
    return (
        token_embed,
        momentum_first,
        variance_first,
        master_first,
        master_first.astype(jnp.bfloat16),
        momentum_second,
        variance_second,
        master_second,
        master_second.astype(jnp.bfloat16),
        momentum_final,
        variance_final,
        master_final,
        master_final.astype(jnp.bfloat16),
        momentum_norm,
        variance_norm,
        master_norm,
        momentum_bias,
        variance_bias,
        master_bias,
    )


def solution(mesh):
    rows = P("ids", None)
    grid = P("ids", "mdl")
    columns = P(None, "mdl")
    mdl_rows = P("mdl", None)
    return jax.shard_map(
        body,
        mesh=mesh,
        in_specs=(grid, rows, P("ids"), P("ids"), rows, grid, columns, mdl_rows, columns, P())
        + (grid,) * 2
        + (columns,) * 2
        + (mdl_rows,) * 2
        + (columns,) * 2
        + (P(),) * 2,
        out_specs=(rows,)
        + (grid,) * 4
        + (columns,) * 4
        + (mdl_rows,) * 4
        + (columns,) * 3
        + (P(),) * 3,
        check_vma=False,
    )
```

time: 1160 us -> 1010 us (0.87)
  other arithmetic: 215 us -> 72.2 us
  blocking collectives: 134 us -> 262 us
  waiting for transfers between devices: 573 us -> 477 us
  local copies, waits for them, and re-layouts: 108 us -> 37.4 us
  matrix products: 93.4 us -> 121 us
    unnamed x7 -> x9, waiting for transfers between devices: 388 us -> 0.15 us
    psum x2, waiting for transfers between devices: 84.9 us -> 264 us  [the longest x1 155 us: body(): grad_second = lax.psum(grad_second, 'ids')]
    reduce_scatter x1 -> x3, waiting for transfers between devices: 57.7 us -> 205 us  [the longest x1 127 us: body(): lax.psum_scatter(local_second, 'mdl', scatter_dimension=0, tiled=False)]
    scatter-add x3 -> x0, other arithmetic: 135 us -> none  [the longest x1 46.6 us: body(): jax.ops.segment_sum(cotangent.astype(jnp.float32) / token_total, token_sl...]
    gather x3 -> x0, local copies, waits for them, and re-layouts: 62.9 us -> none  [the longest x2 33.4 us: body(): jnp.take(embed_low, local_rows, axis=0)]
    psum x4, blocking collectives: 104 us -> 160 us  [the longest x1 40.7 us: body(): lax.psum((jnp.stack([jnp.sum(incoming_one * unit_one, 0), jnp.sum(incomin...]
    all_gather x1 -> x5, blocking collectives: 30.5 us -> 83.5 us  [the longest x1 48.9 us: body(): lax.all_gather(jnp.pad(norm_params, ((0, 0), (0, more))), 'mdl', axis=1,...]
    dot_general x1 -> x5, matrix products: 19 us -> 58.5 us  [the longest x1 18.3 us: body(): jnp.dot(normed_one, second_low, preferred_element_type=jnp.float32)]
  transfers between devices with their start and end apart: 10 -> 12, of which waited for: 6 -> 7; matrix products, arithmetic and copies ran while one was open for 25% -> 12% of each run, Pallas kernels for 0% -> 0%
where the time goes in v1:
time: 1010 us; the launch traced here: 1000 us
  waiting for transfers between devices  477 us (47%)
  blocking collectives  262 us (26%)
  matrix products  121 us (12%)
  other arithmetic  72.2 us (7%)
  local copies, waits for them, and re-layouts  37.4 us (4%)
  between operations  15.7 us (2%)
  starting transfers between devices  15 us (1%)
    psum x1, waiting for transfers between devices, body(): grad_second = lax.psum(grad_second, 'ids')  155 us
    reduce_scatter x1, waiting for transfers between devices, body(): lax.psum_scatter(local_second, 'mdl', scatter_dimension=0, tiled=False)  127 us
    psum x1, waiting for transfers between devices, body(): lax.psum((jnp.stack([jnp.sum(incoming_one * unit_one, 0), jnp.sum(incomin...  110 us
    all_gather x1, blocking collectives, body(): lax.all_gather(jnp.pad(norm_params, ((0, 0), (0, more))), 'mdl', axis=1,...  48.9 us
    reduce_scatter x1, waiting for transfers between devices, body(): lax.psum_scatter(local_first, 'mdl', scatter_dimension=0, tiled=False)  47.1 us
    dot_general x11, matrix products, contract(): lax.dot_general(left, right, (((left_dim,), (right_dim,)), ((), ())), pre...  45.5 us
    psum x1, blocking collectives, body(): lax.psum((jnp.stack([jnp.sum(incoming_one * unit_one, 0), jnp.sum(incomin...  40.7 us
    psum x1, blocking collectives, body(): lax.psum(jnp.stack([jnp.sum(incoming_two * unit_two, 0), jnp.sum(incoming...  40.2 us
  transfers between devices with their start and end apart: 12, of which 7 were waited for; matrix products, arithmetic and copies ran while one was open for 12% of the time, Pallas kernels for 0%

profile of v1, /device:TPU:0, one launch (start us, length us, event | category | flops | bytes accessed | tf_op | source)
XLA Modules:
  0.0 1000.3 jit_solution(2400045335157976259)
XLA Ops:
  9.8 13.0 %subtract_convert_fusion = (bf16[2048,32]{0,1:T(8,128)(2,1)S(1)}, bf16[2048,32]{0,1:T(8,128)(2,1)S(1)}) fusion(bf16[8192,32]{0,1:T(8,128)(2,1)S(1)} %copy-done, s32[8192]{0:T(1024)S(1)} %fusion.37), kind=kOutput, calls=%fused_computation.68 | convolution fusion | flops 1090846720 | bytes 819200 | tf_op jit(solution)/shard_map/dot_general | solution.py:139
  24.0 2.2 reduce.4
  26.4 18.5 %all_to_all.48 = bf16[8,2,8192]{2,1,0:T(2,128)(2,1)S(1)} all-to-all(bf16[8,2,8192]{2,1,0:T(2,128)(2,1)S(1)} %reshape.107), channel_id=1, replica_groups=mesh['ids'=8,'mdl'=4] {'ids'}, dimensions={0} | all-to-all | bytes 524288 | tf_op jit(solution)/shard_map/all_to_all | solution.py:144
  48.2 5.1 all-gather.5.cloned.1.call-done
  53.7 3.4 convert_element_type.79
  57.1 5.6 reshape.96
  66.3 5.0 all-to-all-start
  71.3 4.1 add_convert_fusion.2
  75.4 2.6 all-to-all-done
  78.0 3.7 all-to-all-start.1
  81.7 48.9 %all_gather.27 = f32[4,2048]{1,0:T(4,128)S(1)} all-gather(f32[4,512]{1,0:T(4,128)S(1)} %pad.17), channel_id=1, replica_groups=mesh['ids'=8,'mdl'=4] {'mdl'}, dimensions={1}, use_global_device_ids=true | all-gather | bytes 40960 | tf_op jit(solution)/shard_map/all_gather | solution.py:121
  130.7 5.4 all_gather.32
  136.2 2.4 copy.86
  140.1 6.3 fusion.4
  147.0 11.5 %multiply_reduce_fusion.1 = (f32[2048]{0:T(1024)S(1)}, f32[2048]{0:T(1024)S(1)}, f32[1024,2048]{1,0:T(8,128)}) fusion(f32[1024]{0:T(1024)S(1)} %bitcast.109, bf16[1024,1024]{0,1:T(8,128)(2,1)S(1)} %bitcast.85, bf16[1024,2048]{0,1:T(8,128)(2,1)} %all-gather.7.cloned.1.call-done), kind=kOutput, calls=%fused_computation.19 | convolution fusion | flops 4318031872 | bytes 14700544 | tf_op jit(solution)/shard_map/dot_general | solution.py:158
  158.5 39.1 %all-reduce.6 = (f32[2,2048]{1,0:T(2,128)S(1)}, f32[]{:T(128)}) all-reduce(f32[2,2048]{1,0:T(2,128)S(1)} %pad_maximum_fusion.3, f32[]{:T(128)} %get-tuple-element.151), channel_id=1, replica_groups=mesh['ids'=8,'mdl'=4] {'ids','mdl'}, use_global_device_ids=true, to_apply=%region_2.3 | all-reduce | flops 4097 | bytes 32776 | tf_op jit(solution)/shard_map/psum | solution.py:162
  198.9 7.3 add_convert_fusion.1
  206.2 18.3 %multiply_reduce_fusion = (f32[2048]{0:T(1024)S(1)}, f32[2048]{0:T(1024)S(1)}, f32[1024,2048]{1,0:T(8,128)}, f32[1024,2048]{1,0:T(8,128)}) fusion(f32[1024]{0:T(1024)S(1)} %bitcast.110, bf16[1024,2048]{1,0:T(8,128)(2,1)} %add_convert_fusion.1, bf16[2048,2048]{0,1:T(8,128)(2,1)} %all-gather.11.cloned.1.call-done), kind=kOutput, calls=%fused_computation.17 | convolution fusion | flops 8612999168 | bytes 29380608 | tf_op jit(solution)/shard_map/dot_general | solution.py:167
  224.5 40.1 %psum.58 = f32[2,2048]{1,0:T(2,128)S(1)} all-reduce(f32[2,2048]{1,0:T(2,128)S(1)} %pad_maximum_fusion.4), channel_id=1, replica_groups=mesh['ids'=8,'mdl'=4] {'ids','mdl'}, use_global_device_ids=true, to_apply=%region_7.8 | all-reduce | flops 4096 | bytes 32768 | tf_op jit(solution)/shard_map/psum | solution.py:170
  265.5 5.1 convert_reduce_fusion
  270.6 4.2 multiply_reduce_fusion.3
  274.9 40.2 %psum.59 = f32[2,2048]{1,0:T(2,128)S(1)} all-reduce(f32[2,2048]{1,0:T(2,128)S(1)} %pad_maximum_fusion.5), channel_id=1, replica_groups=mesh['ids'=8,'mdl'=4] {'ids','mdl'}, use_global_device_ids=true, to_apply=%region_10.11 | all-reduce | flops 4096 | bytes 32768 | tf_op jit(solution)/shard_map/psum | solution.py:202
  315.1 12.7 %multiply_convert_fusion.1 = bf16[1024,2048]{1,0:T(8,128)(2,1)S(1)} fusion(f32[1024,2048]{1,0:T(8,128)} %get-tuple-element.167, f32[1024,2048]{1,0:T(8,128)} %get-tuple-element.165, f32[1024,2048]{1,0:T(8,128)} %get-tuple-element.148, f32[]{:T(128)} %get-tuple-element.125, f32[2048]{0:T(1024)S(1)} %bitcast.120, f32[2048]{0:T(1024)S(1)} %bitcast.119, ...), kind=kLoop, calls=%fused_computation.25 | loop fusion | flops 52428800 | bytes 29405188 | tf_op jit(solution)/shard_map/convert_element_type | solution.py:210
  327.8 18.4 %multiply_reduce_fusion.2 = (f32[2048]{0:T(1024)S(1)}, f32[2048]{0:T(1024)S(1)}, f32[1024,2048]{1,0:T(8,128)}) fusion(f32[2048]{0:T(1024)S(1)} %bitcast.94, f32[2048]{0:T(1024)S(1)} %bitcast.97, f32[1024,2048]{1,0:T(8,128)} %get-tuple-element.164, bf16[1024,2048]{1,0:T(8,128)(2,1)S(1)} %multiply_convert_fusion.1, ...), kind=kOutput, calls=%fused_computation.24 | convolution fusion | flops 8615096320 | bytes 29392896 | tf_op jit(solution)/shard_map/dot_general | solution.py:38
  346.2 40.7 %all-reduce.5 = (f32[2,2048]{1,0:T(2,128)S(1)}, f32[32]{0:T(128)S(1)}) all-reduce(f32[2,2048]{1,0:T(2,128)S(1)} %pad_maximum_fusion.6, f32[32]{0:T(128)S(1)} %get-tuple-element.144), channel_id=1, replica_groups=mesh['ids'=8,'mdl'=4] {'ids','mdl'}, use_global_device_ids=true, to_apply=%region_13.14 | all-reduce | flops 4128 | bytes 33024 | tf_op jit(solution)/shard_map/psum | solution.py:221
  386.9 11.3 %multiply_convert_fusion = bf16[1024,2048]{1,0:T(8,128)(2,1)S(1)} fusion(f32[1024,2048]{1,0:T(8,128)} %get-tuple-element.168, f32[1024,2048]{1,0:T(8,128)} %get-tuple-element.164, f32[2048]{0:T(1024)S(1)} %bitcast.114, f32[2048]{0:T(1024)S(1)} %bitcast.113, f32[]{:T(128)} %get-tuple-element.125, f32[2048]{0:T(1024)S(1)} %bitcast.95, f32[2048]{0:T(1024)S(1)} %bitcast.98, ...), kind=kLoop, calls=%fused_computation.23 | loop fusion | flops 54525952 | bytes 21016580 | tf_op jit(solution)/shard_map/convert_element_type | solution.py:232
  403.2 3.7 pad_maximum_fusion.1
  407.2 5.1 convolution_bitcast_fusion
  412.3 2.4 convolution_bitcast_fusion.1
  414.7 2.4 convolution_bitcast_fusion.2
  417.0 2.4 convolution_bitcast_fusion.3
  419.4 6.5 pad_maximum_fusion
  426.1 5.7 fusion.32
  431.8 47.1 %reduce-scatter.4.cloned.1.call-done = f32[1,1024,512]{2,1,0:T(8,128)} async-done(((f32[4,1024,512]{2,1,0:T(8,128)}), f32[1,1024,512]{2,1,0:T(8,128)}) %reduce-scatter.4.cloned.1.call-update) | async-done | bytes 2097168 | tf_op jit(solution)/shard_map/reduce_scatter | solution.py:239
  479.0 127.4 %reduce-scatter.8.cloned.1.call-done = f32[1,2048,512]{2,1,0:T(8,128)} async-done(((f32[4,2048,512]{2,1,0:T(8,128)}), f32[1,2048,512]{2,1,0:T(8,128)}) %reduce-scatter.8.cloned.1.call-update) | async-done | bytes 4194320 | tf_op jit(solution)/shard_map/reduce_scatter | solution.py:217
  607.7 6.0 all_gather.33
  613.7 6.8 fusion.18
  623.3 5.5 all-to-all-start.3
  630.0 109.6 %all-reduce.12.cloned.1.call-done = f32[2048,32]{0,1:T(8,128)} async-done(((f32[2048,32]{0,1:T(8,128)}), f32[2048,32]{0,1:T(8,128)}) %all-reduce.12.cloned.1.call-update) | async-done | bytes 262160 | tf_op jit(solution)/shard_map/psum | solution.py:221
  742.6 15.7 %all_gather.34 = bf16[8,1024,32]{2,1,0:T(8,128)(2,1)S(1)} all-gather(bf16[8,256,32]{2,1,0:T(8,128)(2,1)S(1)} %reshape.98), channel_id=1, replica_groups=mesh['ids'=8,'mdl'=4] {'mdl'}, dimensions={1}, use_global_device_ids=true | all-gather | bytes 655360 | tf_op jit(solution)/shard_map/all_gather | solution.py:188
  758.3 14.1 %fusion.19 = bf16[2048,32]{0,1:T(8,128)(2,1)S(1)} fusion(bf16[8192,32]{1,0:T(8,128)(2,1)S(1)} %bitcast.83, s32[2048]{0:T(1024)S(1)} %dynamic-slice-done), kind=kOutput, calls=%fused_computation.48 | convolution fusion | flops 1090584576 | bytes 663552 | tf_op jit(solution)/shard_map/dot_general | solution.py:195
  772.4 7.5 all_gather.35
  779.9 30.7 %reduce-scatter.6.cloned.1.call-done = f32[128,512]{1,0:T(8,128)} async-done(((f32[1024,512]{1,0:T(8,128)}), f32[128,512]{1,0:T(8,128)}) %reduce-scatter.6.cloned.1.call-update) | async-done | bytes 262160 | tf_op jit(solution)/shard_map/reduce_scatter | solution.py:240
  815.0 154.8 %all-reduce.10.cloned.1.call-done = f32[4,512,512]{2,1,0:T(8,128)} async-done(((f32[4,512,512]{2,1,0:T(8,128)}), f32[4,512,512]{2,1,0:T(8,128)}) %all-reduce.10.cloned.1.call-update) | async-done | bytes 4194320 | tf_op jit(solution)/shard_map/psum | solution.py:218
  969.8 4.3 slice.126
  974.1 4.3 reshape.103
  978.3 5.2 copy.103
  983.5 9.0 fusion.48
  (132 shorter events, 33.7 us)
Async XLA Ops:
  7.2 2.6 copy-start
  7.2 46.1 %all-gather.5.cloned.1.call-start = ((), (), s32[]{:S(2)}) async-start(), calls=%async_computation.7 | async-start | bytes 1179648 | tf_op jit(solution)/shard_map/all_gather | solution.py:112
  9.0 129.6 %all-gather.9.cloned.1.call-start = ((), (), s32[]{:S(2)}) async-start(), calls=%async_computation.9 | async-start | bytes 1310720 | tf_op jit(solution)/shard_map/all_gather | solution.py:145
  48.2 98.8 %all-gather.7.cloned.1.call-start = ((), (), s32[]{:S(2)}) async-start(), calls=%async_computation.8 | async-start | bytes 5242880 | tf_op jit(solution)/shard_map/all_gather | solution.py:113
  53.3 12.3 %copy-start.17 = (s32[8,1024]{1,0:T(8,128)S(1)}, s32[8,1024]{1,0:T(8,128)}, u32[]{:S(2)}) copy-start(s32[8,1024]{1,0:T(8,128)} %param.21) | copy-start | bytes 98308
  53.3 12.3 %copy-start.20 = (s32[8]{0:T(128)S(1)}, s32[8]{0:T(128)}, u32[]{:S(2)}) copy-start(s32[8]{0:T(128)} %param.22) | copy-start | bytes 100
  53.3 152.9 %all-gather.11.cloned.1.call-start = ((), (), s32[]{:S(2)}) async-start(), calls=%async_computation.10 | async-start | bytes 10485760 | tf_op jit(solution)/shard_map/all_gather | solution.py:118
  63.5 18.1 %copy-start.8 = (f32[450,32]{0,1:T(8,128)S(1)}, f32[450,32]{0,1:T(8,128)}, u32[]{:S(2)}) copy-start(f32[450,32]{0,1:T(8,128)} %param.27) | copy-start | bytes 172804
  63.5 18.2 %copy-start.15 = (f32[4,450]{1,0:T(4,128)S(1)}, f32[4,450]{1,0:T(4,128)}, u32[]{:S(2)}) copy-start(f32[4,450]{1,0:T(4,128)} %param.28) | copy-start | bytes 21604
  66.3 11.7 %all-to-all-start = ((s32[8,1,1024]{2,1,0:T(1,128)}), s32[8,1,1024]{2,1,0:T(1,128)S(1)}, u32[]{:S(2)}, u32[]{:S(2)}) async-start(s32[8,1,1024]{2,1,0:T(1,128)} %all_to_all.32), calls=%async_computation | async-start | bytes 65536 | tf_op jit(solution)/shard_map/all_to_all | solution.py:132
  78.0 68.4 %copy-start.12 = (s32[8,1,1024]{2,1,0:T(1,128)}, s32[8,1,1024]{2,1,0:T(1,128)S(1)}, u32[]{:S(2)}) copy-start(s32[8,1,1024]{2,1,0:T(1,128)S(1)} %all-to-all-done) | copy-start | bytes 98308
  78.0 58.2 %all-to-all-start.1 = ((bf16[4,1024,256]{2,1,0:T(8,128)(2,1)}), bf16[4,1024,256]{2,1,0:T(8,128)(2,1)S(1)}, u32[]{:S(2)}, u32[]{:S(2)}) async-start(bf16[4,1024,256]{2,1,0:T(8,128)(2,1)} %bitcast.3), calls=%async_computation.1 | async-start | bytes 4194304 | tf_op jit(solution)/shard_map/all_to_all | solution.py:124
  81.6 397.3 %reduce-scatter.4.cloned.1.call-start = ((), (), s32[]{:S(2)}) async-start(), calls=%async_computation.11 | async-start | bytes 10485760 | tf_op jit(solution)/shard_map/reduce_scatter | solution.py:239
  140.1 6.9 copy-start.6
  206.2 59.3 %copy-start.21 = (f32[32]{0:T(128)S(1)}, f32[32]{0:T(128)}, u32[]{:S(2)}) copy-start(f32[32]{0:T(128)} %param.29) | copy-start | bytes 388
  264.7 6.0 copy-start.2
  327.8 18.4 %copy-start.4 = (bf16[1024,2048]{1,0:T(8,128)(2,1)}, bf16[1024,2048]{1,0:T(8,128)(2,1)S(1)}, u32[]{:S(2)}) copy-start(bf16[1024,2048]{1,0:T(8,128)(2,1)S(1)} %multiply_convert_fusion.1) | copy-start | bytes 12582916
  406.9 199.5 %reduce-scatter.8.cloned.1.call-start = ((), (), s32[]{:S(2)}) async-start(), calls=%async_computation.13 | async-start | bytes 20971520 | tf_op jit(solution)/shard_map/reduce_scatter | solution.py:217
  407.1 5.1 copy-start.3
  407.1 5.1 copy-start.5
  426.0 180.5 %copy-start.7 = (f32[128,450]{0,1:T(8,128)S(1)}, f32[128,450]{0,1:T(8,128)}, u32[]{:S(2)}) copy-start(f32[128,450]{0,1:T(8,128)} %param.25) | copy-start | bytes 691204
  426.0 180.7 %copy-start.10 = (f32[128,450]{0,1:T(8,128)S(1)}, f32[128,450]{0,1:T(8,128)}, u32[]{:S(2)}) copy-start(f32[128,450]{0,1:T(8,128)} %param.31) | copy-start | bytes 691204
  426.0 180.8 %copy-start.11 = (f32[128,450]{0,1:T(8,128)S(1)}, f32[128,450]{0,1:T(8,128)}, u32[]{:S(2)}) copy-start(f32[128,450]{0,1:T(8,128)} %param.30) | copy-start | bytes 691204
  426.0 313.6 %all-reduce.12.cloned.1.call-start = ((), (), s32[]{:S(2)}) async-start(), calls=%async_computation.15 | async-start | bytes 524288 | tf_op jit(solution)/shard_map/psum | solution.py:221
  431.8 378.8 %reduce-scatter.6.cloned.1.call-start = ((), (), s32[]{:S(2)}) async-start(), calls=%async_computation.12 | async-start | bytes 2359296 | tf_op jit(solution)/shard_map/reduce_scatter | solution.py:240
  478.9 490.8 %all-reduce.10.cloned.1.call-start = ((), (), s32[]{:S(2)}) async-start(), calls=%async_computation.14 | async-start | bytes 8388608 | tf_op jit(solution)/shard_map/psum | solution.py:218
  606.6 22.2 %copy-start.22 = (f32[32]{0:T(128)S(1)}, f32[32]{0:T(128)}, u32[]{:S(2)}) copy-start(f32[32]{0:T(128)} %param.39) | copy-start | bytes 388
  606.6 22.2 %copy-start.23 = (f32[32]{0:T(128)S(1)}, f32[32]{0:T(128)}, u32[]{:S(2)}) copy-start(f32[32]{0:T(128)} %param.38) | copy-start | bytes 388
  606.6 22.7 %copy-start.16 = (f32[4,450]{1,0:T(4,128)S(1)}, f32[4,450]{1,0:T(4,128)}, u32[]{:S(2)}) copy-start(f32[4,450]{1,0:T(4,128)} %param.28) | copy-start | bytes 21604
  606.6 22.7 %copy-start.18 = (f32[4,450]{1,0:T(4,128)S(1)}, f32[4,450]{1,0:T(4,128)}, u32[]{:S(2)}) copy-start(f32[4,450]{1,0:T(4,128)} %param.37) | copy-start | bytes 21604
  606.6 22.7 %copy-start.19 = (f32[4,450]{1,0:T(4,128)S(1)}, f32[4,450]{1,0:T(4,128)}, u32[]{:S(2)}) copy-start(f32[4,450]{1,0:T(4,128)} %param.36) | copy-start | bytes 21604
  606.7 133.0 %copy-start.9 = (f32[450,32]{0,1:T(8,128)S(1)}, f32[450,32]{0,1:T(8,128)}, u32[]{:S(2)}) copy-start(f32[450,32]{0,1:T(8,128)} %param.27) | copy-start | bytes 172804
  606.7 133.0 %copy-start.13 = (f32[450,32]{0,1:T(8,128)S(1)}, f32[450,32]{0,1:T(8,128)}, u32[]{:S(2)}) copy-start(f32[450,32]{0,1:T(8,128)} %param.35) | copy-start | bytes 172804
  606.7 133.0 %copy-start.14 = (f32[450,32]{0,1:T(8,128)S(1)}, f32[450,32]{0,1:T(8,128)}, u32[]{:S(2)}) copy-start(f32[450,32]{0,1:T(8,128)} %param.34) | copy-start | bytes 172804
  613.7 144.6 %dynamic-slice-start = ((s32[8192]{0:T(1024)}, s32[]{:T(128)}), s32[2048]{0:T(1024)S(1)}, s32[]{:S(2)}) async-start(s32[8192]{0:T(1024)} %param.23, s32[]{:T(128)} %select_n.30), calls=%async_computation.16 | async-start | bytes 16896 | tf_op jit(solution)/shard_map/dynamic_slice | solution.py:190
  623.3 118.1 %all-to-all-start.3 = ((bf16[8,2,4096]{2,1,0:T(2,128)(2,1)}), bf16[8,2,4096]{2,1,0:T(2,128)(2,1)S(1)}, u32[]{:S(2)}, u32[]{:S(2)}) async-start(bf16[8,2,4096]{2,1,0:T(2,128)(2,1)} %reshape.109), calls=%async_computation.3 | async-start | bytes 262144 | tf_op jit(solution)/shard_map/all_to_all | solution.py:187
  978.3 14.9 %copy-start.1 = (bf16[8192,32]{0,1:T(8,128)(2,1)S(1)}, bf16[8192,32]{0,1:T(8,128)(2,1)}, u32[]{:S(2)}) copy-start(bf16[8192,32]{0,1:T(8,128)(2,1)} %param.24) | copy-start | bytes 1572868
Sparse Core Ops, SparseCore 0:
  10.6 42.5 all-gather.4
  55.4 17.2 all-gather.8
  74.3 56.9 all-gather.6
  133.3 57.1 all-gather.10
  407.0 71.8 reduce-scatter.3
  481.3 125.0 reduce-scatter.7
  612.5 127.0 all-reduce.11
  743.2 67.4 reduce-scatter.5
  814.3 155.4 all-reduce.9

commit v2 on v1

v2 whole, which is shorter than its diff:
```python
import functools
import jax
import jax.numpy as jnp
from jax import lax
from jax.experimental import pallas as pl
from jax.experimental.pallas import tpu as pltpu
from jax.sharding import PartitionSpec as P

STEP = 10


beta_one = 0.9
beta_two = 0.999
adam_epsilon = 1e-08
norm_epsilon = 1e-05
penalty_weight = 0.25
decay_matrix = 0.01
rate_matrix = 0.05
rate_norm = 0.5
rate_bias = 0.02
LANES = 128


def mish_parts(inputs):
    grown = jnp.exp(jnp.minimum(inputs, 20.0))
    above = grown * (grown + 2.0)
    inverse = 1.0 / (above + 2.0)
    return grown, above * inverse, inverse


def mish(inputs):
    return inputs * mish_parts(inputs)[1]


def mish_slope(inputs):
    grown, gate, inverse = mish_parts(inputs)
    return gate + 4.0 * jnp.minimum(inputs, 20.0) * (grown * inverse) * ((1.0 + grown) * inverse)


def contract(left, right, left_dim, right_dim):
    return lax.dot_general(
        left, right, (((left_dim,), (right_dim,)), ((), ())), preferred_element_type=jnp.float32
    )


def norm_back(upstream, unit_rows, gain_row, scale_row, live_mask, gain_sum, shift_sum, live_count):
    return scale_row * (
        gain_row * upstream
        - live_mask[:, None] * gain_row * (shift_sum + unit_rows * gain_sum) / live_count
    )


def adam(weight, moment, square, gradient, step_rate, shrink):
    momentum = beta_one * moment + (1.0 - beta_one) * gradient
    variance = beta_two * square + (1.0 - beta_two) * gradient * gradient
    moment_hat = momentum / (1.0 - beta_one**STEP)
    square_hat = variance / (1.0 - beta_two**STEP)
    master = weight - step_rate * (
        moment_hat / (jnp.sqrt(square_hat) + adam_epsilon) + shrink * weight
    )
    return (momentum, variance, master)


def split_two(values):
    high = values.astype(jnp.bfloat16)
    low = (values - high.astype(jnp.float32)).astype(jnp.bfloat16)
    return high, low


def one_hot(index, length, first):
    rows = lax.broadcasted_iota(jnp.int32, (length, index.shape[0]), 0) + first
    return (rows == index[None, :]).astype(jnp.bfloat16)


MESH = pl.DeviceIdType.MESH
BIG = 60 * 1024 * 1024


def greet(peers):
    barrier = pltpu.get_barrier_semaphore()
    for peer in peers:
        pl.semaphore_signal(barrier, inc=1, device_id=peer, device_id_type=MESH)
    pl.semaphore_wait(barrier, len(peers))


def push(source, target, send_sem, recv_sem, peer):
    return pltpu.make_async_remote_copy(
        src_ref=source,
        dst_ref=target,
        send_sem=send_sem,
        recv_sem=recv_sem,
        device_id=peer,
        device_id_type=MESH,
    )


def gap(axis, size, d):
    return {axis: lax.rem(lax.axis_index(axis) + d, size)}


def exchange_kernel(parts, owners, kinds, *refs):
    extras = len(kinds)
    x_ref, given = refs[0], refs[1 : 1 + extras]
    o_ref, taken = refs[1 + extras], refs[2 + extras : 2 + 2 * extras]
    near, far, send_near, recv_near, send_far, recv_far, *sems = refs[2 + 2 * extras :]
    sizes = {"mdl": parts, "ids": owners}
    part = lax.axis_index("mdl")
    owner = lax.axis_index("ids")
    greet([gap("mdl", parts, d) for d in range(1, parts)] + [gap("ids", owners, d) for d in range(1, owners)])
    copies = [
        push(x_ref, near.at[d], send_near.at[d], recv_near.at[d], gap("mdl", parts, d))
        for d in range(1, parts)
    ]
    for copy in copies:
        copy.start()
    others = []
    for n, (axis, spread) in enumerate(kinds):
        me = lax.axis_index(axis)
        for d in range(1, sizes[axis]):
            peer = gap(axis, sizes[axis], d)
            source = given[n].at[peer[axis]] if spread else given[n]
            copy = push(source, taken[n].at[me], sems[2 * n].at[d], sems[2 * n + 1].at[d], peer)
            copy.start()
            others.append(copy)
        taken[n][me] = given[n][me] if spread else given[n][...]
    near[0] = x_ref[...]
    for copy in copies:
        copy.wait()
    total = near[part]
    for k in range(1, parts):
        total = total + near[lax.rem(part + parts - k, parts)]
    far[0] = total
    copies = [
        push(far.at[0], far.at[d], send_far.at[d], recv_far.at[d], gap("ids", owners, d))
        for d in range(1, owners)
    ]
    for copy in copies:
        copy.start()
    for copy in copies:
        copy.wait()
    total = far[owner]
    for k in range(1, owners):
        total = total + far[lax.rem(owner + owners - k, owners)]
    o_ref[...] = total
    for copy in others:
        copy.wait()


def exchange(x, extras, kinds, call):
    parts, owners = lax.axis_size("mdl"), lax.axis_size("ids")
    sizes = {"mdl": parts, "ids": owners}
    dma = pltpu.SemaphoreType.DMA
    whole = pl.BlockSpec(memory_space=pltpu.VMEM)
    outs = [jax.ShapeDtypeStruct(x.shape, jnp.float32)]
    sems = []
    for extra, (axis, spread) in zip(extras, kinds):
        shape = extra.shape if spread else (sizes[axis],) + extra.shape
        outs.append(jax.ShapeDtypeStruct(shape, extra.dtype))
        sems += [dma((sizes[axis],)), dma((sizes[axis],))]
    return pl.pallas_call(
        functools.partial(exchange_kernel, parts, owners, kinds),
        out_shape=tuple(outs),
        in_specs=[whole] * (1 + len(extras)),
        out_specs=(whole,) * len(outs),
        scratch_shapes=[
            pltpu.VMEM((parts,) + x.shape, jnp.float32),
            pltpu.VMEM((owners,) + x.shape, jnp.float32),
            dma((parts,)),
            dma((parts,)),
            dma((owners,)),
            dma((owners,)),
        ]
        + sems,
        compiler_params=pltpu.CompilerParams(collective_id=call, has_side_effects=True),
        name="exchange",
    )(x, *extras)


def front_kernel(
    parts, owners, first, codes, norms, final, wanted, weights, feats, norms_all, final_all, received,
    s1, r1, s2, r2, s3, r3, sc, rc, sn, rn, sw, rw, sl,
):
    part = lax.axis_index("mdl")
    owner = lax.axis_index("ids")
    pair = {"mdl": part + 1 - 2 * lax.rem(part, 2)}
    cross_part = lax.rem(part + 2, parts)
    cross = {"mdl": cross_part}
    rows, width = first.shape
    codes_width = codes.shape[2]
    greet([gap("mdl", parts, d) for d in range(1, parts)] + [gap("ids", owners, d) for d in range(1, owners)])

    def spot(who, which):
        return weights.at[
            pl.ds(pl.multiple_of(who * rows, rows), rows),
            pl.ds(pl.multiple_of(which * width, width), width),
        ]

    mine = feats.at[:, pl.ds(pl.multiple_of(part * codes_width, codes_width), codes_width)]
    locals_ = [
        pltpu.make_async_copy(first, spot(owner, part), sl.at[0]),
        pltpu.make_async_copy(codes.at[part], mine, sl.at[1]),
    ]
    for copy in locals_:
        copy.start()
    ones, lines = [], []
    for d in range(1, owners):
        peer = gap("ids", owners, d)
        copy = push(first, spot(owner, part), s1.at[d], r1.at[d], peer)
        copy.start()
        ones.append(copy)
        copy = push(wanted.at[peer["ids"]], received.at[owner], sw.at[d], rw.at[d], peer)
        copy.start()
        lines.append(copy)
    for d in range(1, parts):
        peer = gap("mdl", parts, d)
        for n, (source, target) in enumerate(((norms, norms_all), (final, final_all))):
            copy = push(source, target.at[part], sn.at[n, d], rn.at[n, d], peer)
            copy.start()
            lines.append(copy)
    for d in range(1, parts):
        peer = gap("mdl", parts, d)
        copy = push(codes.at[peer["mdl"]], mine, sc.at[d], rc.at[d], peer)
        copy.start()
        lines.append(copy)
    received[owner] = wanted[owner]
    norms_all[part] = norms[...]
    final_all[part] = final[...]
    twos, threes = [], []
    for d in range(owners):
        who = lax.rem(owner + owners - d, owners)
        if d == 0:
            locals_[0].wait()
        else:
            ones[d - 1].wait_send()
            push(first, spot(who, part), s1.at[d], r1.at[d], pair).wait_recv()
        piece = spot(who, part)
        copy = push(piece, piece, s2.at[d], r2.at[d], cross)
        copy.start()
        twos.append(copy)
        copy = push(piece, piece, s3.at[0, d], r3.at[0, d], pair)
        copy.start()
        threes.append(copy)
    for d in range(owners):
        who = lax.rem(owner + owners - d, owners)
        twos[d].wait_send()
        piece = spot(who, cross_part)
        push(piece, piece, s2.at[d], r2.at[d], cross).wait_recv()
        copy = push(piece, piece, s3.at[1, d], r3.at[1, d], pair)
        copy.start()
        threes.append(copy)
    for copy in threes + lines:
        copy.wait()
    locals_[1].wait()


def front(first, codes, norms, final, wanted, call):
    parts, owners = lax.axis_size("mdl"), lax.axis_size("ids")
    dma = pltpu.SemaphoreType.DMA
    held = pl.BlockSpec(memory_space=pl.ANY)
    whole = pl.BlockSpec(memory_space=pltpu.VMEM)
    shape = jax.ShapeDtypeStruct
    return pl.pallas_call(
        functools.partial(front_kernel, parts, owners),
        out_shape=(
            shape((first.shape[0] * owners, first.shape[1] * parts), first.dtype),
            shape((codes.shape[1], codes.shape[2] * parts), codes.dtype),
            shape((parts,) + norms.shape, norms.dtype),
            shape((parts,) + final.shape, final.dtype),
            shape(wanted.shape, wanted.dtype),
        ),
        in_specs=[whole] * 5,
        out_specs=(held, held, whole, whole, whole),
        scratch_shapes=[dma((owners,))] * 4
        + [dma((2, owners))] * 2
        + [dma((parts,))] * 2
        + [dma((2, parts))] * 2
        + [dma((owners,))] * 2
        + [dma((2,))],
        compiler_params=pltpu.CompilerParams(collective_id=call, has_side_effects=True, vmem_limit_bytes=16 * 1024 * 1024),
        name="front",
    )(first, codes, norms, final, wanted)


def blocks(count, step, body):
    if count == step:
        body(0)
    else:
        @pl.loop(0, count // step)
        def _(k):
            body(pl.multiple_of(k * step, step))


NAMES = (
    "own",
    "got",
    "out_y",
    "in_y",
    "out_f",
    "in_f",
    "s0",
    "r0",
    "sl",
    "sy",
    "ry",
    "sf",
    "rf",
    "sg",
    "rg",
    "st",
    "rt",
)


class Unit:
    pass


def reduce_kernel(parts, owners, plan, *refs):
    half = parts // 2
    count = len(plan)
    inputs, (replies, picks) = refs[:count], refs[count : count + 2]
    outputs, tokens_out = refs[count + 2 : 2 * count + 2], refs[2 * count + 2]
    scratch = list(refs[2 * count + 3 :])
    gathered, made, sp, rp, st_, rt_ = scratch[:6]
    scratch = scratch[6:]
    part = lax.axis_index("mdl")
    owner = lax.axis_index("ids")
    low, place = lax.rem(part, 2), part // 2
    pair = {"mdl": part + 1 - 2 * low}
    cross = {"mdl": lax.rem(part + 2, parts)}
    side, row = lax.rem(owner, 2), owner // 2
    twin = {"ids": owner + 1 - 2 * side}
    line = owners // 2
    units = []
    for n, (rows, lanes, chunks, keep, wire) in enumerate(plan):
        bufs = {name: scratch.pop(0) for name in NAMES[: 17 if keep else 13]}
        for c in range(chunks):
            u = Unit()
            u.__dict__.update(bufs)
            u.rows, u.lanes, u.width, u.keep, u.c, u.wire = rows, lanes, lanes // chunks, keep, c, wire
            u.piece = rows // owners
            u.cols = pl.ds(c * u.width, u.width)
            u.source, u.out = inputs[n], outputs[n]
            units.append(u)
    greet([gap("mdl", parts, d) for d in range(1, parts)] + [gap("ids", owners, d) for d in range(1, owners)])

    def taken(u, k):
        if len(u.source.shape) == 3:
            return u.source.at[k, :, u.cols]
        start = pl.multiple_of(k * u.lanes + u.c * u.width, u.width)
        return u.source.at[:, pl.ds(start, u.width)]

    def begin(u):
        u.first, u.mine = [], []
        for i in range(half):
            u.first.append(
                push(
                    taken(u, 1 - low + 2 * i),
                    u.got.at[i, :, u.cols],
                    u.s0.at[u.c, i],
                    u.r0.at[u.c, i],
                    pair,
                )
            )
            u.mine.append(
                pltpu.make_async_copy(
                    taken(u, low + 2 * i), u.own.at[i, :, u.cols], u.sl.at[u.c, i]
                )
            )
        for copy in u.first + u.mine:
            copy.start()

    def sweep(u, body):
        step = min(u.rows, 64)
        blocks(u.rows, step, lambda k: body((pl.ds(k, step), u.cols)))

    def to_cross(u):
        for copy in u.first + u.mine:
            copy.wait()

        def body(at):
            spot = (1 - place,) + at
            u.out_y[at] = (u.own[spot] + u.got[spot]).astype(u.wire)

        sweep(u, body)
        u.second = push(
            u.out_y.at[:, u.cols], u.in_y.at[:, u.cols], u.sy.at[u.c], u.ry.at[u.c], cross
        )
        u.second.start()

    def to_owners(u):
        u.second.wait()

        def body(at):
            spot = (place,) + at
            value = u.own[spot] + u.got[spot] + u.in_y[at].astype(jnp.float32)
            u.own[spot] = value
            u.out_f[at] = value.astype(u.wire)

        sweep(u, body)
        u.third = []
        for d in range(1, owners):
            peer = lax.rem(owner + d, owners)
            copy = push(
                u.out_f.at[pl.ds(pl.multiple_of(peer * u.piece, u.piece), u.piece), u.cols],
                u.in_f.at[d, :, u.cols],
                u.sf.at[u.c, d],
                u.rf.at[u.c, d],
                {"ids": peer},
            )
            copy.start()
            u.third.append(copy)

    def finish(u):
        for copy in u.third:
            copy.wait()
        here = pl.ds(pl.multiple_of(owner * u.piece, u.piece), u.piece)
        value = u.own[place, here, u.cols]
        for d in range(1, owners):
            value = value + u.in_f[d, :, u.cols].astype(jnp.float32)
        if not u.keep:
            u.out[:, u.cols] = value
            return
        u.out[row, side, :, u.cols] = value
        u.fourth = []
        spot = u.out.at[row, side, :, u.cols]
        for d in range(1, line):
            peer = {"ids": lax.rem(row + d, line) * 2 + side}
            copy = push(spot, spot, u.sg.at[u.c, d], u.rg.at[u.c, d], peer)
            copy.start()
            u.fourth.append(copy)

    def to_twin(u):
        if not u.keep:
            return
        for d, copy in zip(range(1, line), u.fourth):
            copy.wait_send()
            there = u.out.at[lax.rem(row + line - d, line), side, :, u.cols]
            push(there, there, u.sg.at[u.c, d], u.rg.at[u.c, d], twin).wait_recv()
        spot = u.out.at[:, side, :, u.cols]
        u.fifth = push(spot, spot, u.st.at[u.c], u.rt.at[u.c], twin)
        u.fifth.start()

    def close(u):
        if not u.keep:
            return
        u.fifth.wait_send()
        there = u.out.at[:, 1 - side, :, u.cols]
        push(there, there, u.st.at[u.c], u.rt.at[u.c], twin).wait_recv()

    def share(source, target, send, recv):
        copies = [
            push(source, target.at[part], send.at[d], recv.at[d], gap("mdl", parts, d))
            for d in range(1, parts)
        ]
        for copy in copies:
            copy.start()
        return copies

    piece = replies.shape[2]
    slots = piece * parts

    def select(q):
        def body(j, summed):
            first = j * slots + q * piece
            place_ = lax.broadcasted_iota(jnp.int32, (piece, picks.shape[1]), 0) + first
            chosen = jnp.where(place_ == picks[...], 1.0, 0.0).astype(jnp.bfloat16)
            return summed + jnp.dot(gathered[q, j], chosen, preferred_element_type=jnp.float32)

        start = jnp.zeros((replies.shape[1], picks.shape[1]), jnp.float32)
        summed = lax.fori_loop(0, owners, body, start)
        made[...] = summed.astype(jnp.bfloat16) if q == 0 else made[...] + summed.astype(jnp.bfloat16)

    early = share(replies, gathered, sp, rp)
    gathered[part] = replies[...]
    for u in units:
        begin(u)
    total = len(units)
    late = []
    stages = (to_cross, to_owners, finish, to_twin, close)
    for t in range(total + len(stages) - 1):
        for s, stage in enumerate(stages):
            if 0 <= t - s < total:
                stage(units[t - s])
        if t == 0:
            for copy in early:
                copy.wait()
        if t < parts:
            select(t)
        if t == parts - 1:
            tokens_out[part] = made[...]
            late = share(made, tokens_out, st_, rt_)
    for copy in late:
        copy.wait()


def reduce_grads(arrays, plan, replies, picks, call):
    parts, owners = lax.axis_size("mdl"), lax.axis_size("ids")
    half = parts // 2
    found_shape = (replies.shape[1], picks.shape[1])
    outs = []
    scratch = [
        pltpu.VMEM((parts,) + replies.shape, replies.dtype),
        pltpu.VMEM(found_shape, replies.dtype),
    ] + [pltpu.SemaphoreType.DMA((parts,))] * 4
    for rows, lanes, chunks, keep, wire in plan:
        piece = rows // owners
        outs.append(
            jax.ShapeDtypeStruct(
                (owners // 2, 2, piece, lanes) if keep else (piece, lanes), jnp.float32
            )
        )
        dma = pltpu.SemaphoreType.DMA
        scratch += [
            pltpu.VMEM((half, rows, lanes), jnp.float32),
            pltpu.VMEM((half, rows, lanes), jnp.float32),
            pltpu.VMEM((rows, lanes), wire),
            pltpu.VMEM((rows, lanes), wire),
            pltpu.VMEM((rows, lanes), wire),
            pltpu.VMEM((owners, piece, lanes), wire),
            dma((chunks, half)),
            dma((chunks, half)),
            dma((chunks, half)),
            dma((chunks,)),
            dma((chunks,)),
            dma((chunks, owners)),
            dma((chunks, owners)),
        ]
        if keep:
            scratch += [
                dma((chunks, owners // 2)),
                dma((chunks, owners // 2)),
                dma((chunks,)),
                dma((chunks,)),
            ]
    found = pl.pallas_call(
        functools.partial(reduce_kernel, parts, owners, plan),
        out_shape=tuple(outs) + (jax.ShapeDtypeStruct((parts,) + found_shape, replies.dtype),),
        in_specs=[pl.BlockSpec(memory_space=pl.ANY)] * len(arrays)
        + [pl.BlockSpec(memory_space=pltpu.VMEM)] * 2,
        out_specs=(pl.BlockSpec(memory_space=pltpu.VMEM),) * (len(arrays) + 1),
        scratch_shapes=scratch,
        compiler_params=pltpu.CompilerParams(
            collective_id=call, has_side_effects=True, vmem_limit_bytes=BIG
        ),
        name="reduce_grads",
    )(*arrays, replies, picks)
    return tuple(v.reshape(-1, v.shape[-1]) for v in found[:-1]) + (found[-1],)


def total(vectors, small, extras, kinds, call):
    rows = [v.reshape(-1, LANES) for v in vectors]
    sizes = [r.shape[0] for r in rows]
    if small is not None:
        rows.append(jnp.pad(small.reshape(1, -1), ((0, 7), (0, LANES - small.size))))
    summed, *moved = exchange(jnp.concatenate(rows, axis=0), extras, kinds, call)
    found, start = [], 0
    for size in sizes:
        found.append(summed[start : start + size].reshape(-1))
        start += size
    if small is not None:
        found.append(summed[start, : small.size])
    return found, moved


def body(
    hash_codes,
    request_ids,
    request_counts,
    token_slots,
    cotangent,
    weight_first,
    weight_second,
    weight_final,
    norm_params,
    bias_final,
    moment_first,
    square_first,
    moment_second,
    square_second,
    moment_final,
    square_final,
    moment_norm,
    square_norm,
    moment_bias,
    square_bias,
):
    owners = lax.axis_size("ids")
    parts = lax.axis_size("mdl")
    part = lax.axis_index("mdl")
    range_rows = hash_codes.shape[0]
    rows = range_rows // parts
    slots_per = request_ids.shape[1]
    piece = slots_per // parts
    out_width = weight_final.shape[1]
    width = weight_first.shape[1]
    wide = width + (-width) % LANES
    hidden = wide * parts
    more = wide - width
    token_count = token_slots.shape[0]
    token_piece = token_count // parts
    token_total = token_count * owners

    encoded = ((hash_codes.astype(jnp.float32) + 0.5) / 512.0 - 1.0).astype(jnp.bfloat16)
    owner_row = jnp.arange(owners, dtype=jnp.int32)[:, None]
    wanted = jnp.where(
        jnp.arange(slots_per, dtype=jnp.int32)[None, :] < request_counts[:, None],
        request_ids - owner_row * range_rows,
        range_rows,
    )
    first_low, features, norm_all, final_all, received = front(
        jnp.pad(weight_first.astype(jnp.bfloat16), ((0, 0), (0, more))),
        encoded.reshape(parts, rows, -1),
        jnp.pad(norm_params, ((0, 4), (0, more))),
        jnp.pad(weight_final.astype(jnp.bfloat16).T, ((0, 0), (0, more))),
        wanted.reshape(owners, 1, slots_per),
        5,
    )
    norm_all = norm_all.transpose(1, 0, 2).reshape(-1, hidden)[:4]
    final_low = final_all.transpose(1, 0, 2).reshape(out_width, hidden)
    second_part = jnp.pad(
        weight_second.astype(jnp.bfloat16).reshape(parts, width, width),
        ((0, 0), (0, more), (0, more)),
    ).reshape(hidden, wide)
    second_part, first_low = lax.optimization_barrier((second_part, first_low))
    second_low = lax.all_gather(second_part, "mdl", axis=1, tiled=True)

    received = received.reshape(owners, slots_per)
    here = part * rows + jnp.arange(rows, dtype=jnp.int32)
    live_mask = jnp.max(
        (received.reshape(1, -1) == here[:, None]).astype(jnp.float32), axis=1
    )
    slots_mine = lax.dynamic_slice(received, (0, part * piece), (owners, piece)).reshape(-1)
    pick_rows = (
        slots_mine[:, None] == lax.broadcasted_iota(jnp.int32, (owners * piece, range_rows), 1)
    ).astype(jnp.bfloat16)

    slot_owner = token_slots // slots_per
    slot_place = token_slots % slots_per - part * piece
    slot_here = jnp.where(
        (slot_place >= 0) & (slot_place < piece), slot_owner * piece + slot_place, -1
    )
    slot_sum = contract(cotangent, one_hot(slot_here, owners * piece, 0), 0, 1) / token_total
    sent = jnp.concatenate(split_two(slot_sum), axis=0)
    sent = sent.reshape(2 * out_width, owners, piece).transpose(1, 0, 2)

    linear_one = jnp.dot(features, first_low, preferred_element_type=jnp.float32)
    active_one = mish(linear_one)
    weighted_one = live_mask[:, None] * active_one
    (*sums_one, live_count), (arrived,) = total(
        [jnp.sum(weighted_one, 0), jnp.sum(weighted_one * active_one, 0)],
        jnp.sum(live_mask).reshape(1),
        [sent],
        (("ids", True),),
        0,
    )
    live_count = live_count[0]
    mean_one = sums_one[0] / live_count
    scale_one = lax.rsqrt(sums_one[1] / live_count - mean_one * mean_one + norm_epsilon)
    unit_one = (active_one - mean_one) * scale_one
    normed_one = (norm_all[0] * unit_one + norm_all[1]).astype(jnp.bfloat16)
    arrived = arrived.transpose(1, 0, 2).reshape(2 * out_width, owners * piece)
    row_part = jnp.dot(arrived, pick_rows, preferred_element_type=jnp.float32)
    row_part = (row_part[:out_width] + row_part[out_width:]).reshape(out_width, parts, rows)
    linear_two = jnp.dot(normed_one, second_low, preferred_element_type=jnp.float32)
    active_two = mish(linear_two)
    weighted_two = live_mask[:, None] * active_two
    sums_two, (row_parts,) = total(
        [jnp.sum(weighted_two, 0), jnp.sum(weighted_two * active_two, 0)],
        None,
        [row_part.transpose(1, 0, 2)],
        (("mdl", True),),
        1,
    )
    row_grad = jnp.sum(row_parts, 0)
    mean_two = sums_two[0] / live_count
    scale_two = lax.rsqrt(sums_two[1] / live_count - mean_two * mean_two + norm_epsilon)
    unit_two = (active_two - mean_two) * scale_two
    normed_two = (norm_all[2] * unit_two + norm_all[3]).astype(jnp.bfloat16)
    embedding = contract(final_low, normed_two, 1, 1) + bias_final[:, None]

    grad_embed = (
        row_grad + 2.0 * penalty_weight / live_count * live_mask[None, :] * embedding
    ).astype(jnp.bfloat16)
    incoming_two = contract(grad_embed, final_low, 0, 0)
    (*sums_two, grad_bias), (embed_range,) = total(
        [jnp.sum(incoming_two * unit_two, 0), jnp.sum(incoming_two, 0)],
        jnp.sum(grad_embed.astype(jnp.float32), 1),
        [embedding.astype(jnp.bfloat16)],
        (("mdl", False),),
        2,
    )
    embed_range = embed_range.transpose(1, 0, 2).reshape(out_width, range_rows)
    replies = contract(embed_range, pick_rows, 1, 1).astype(jnp.bfloat16)
    replies = replies.reshape(out_width, owners, piece).transpose(1, 0, 2)
    local_final = jnp.pad(
        contract(normed_two, grad_embed, 0, 1).reshape(parts, wide, out_width),
        ((0, 0), (0, 0), (0, (-out_width) % LANES)),
    )
    outgoing_two = norm_back(
        incoming_two, unit_two, norm_all[2], scale_two, live_mask, sums_two[0], sums_two[1], live_count
    )
    grad_linear_two = (mish_slope(linear_two) * outgoing_two).astype(jnp.bfloat16)
    local_second = contract(grad_linear_two, normed_one, 0, 0).reshape(parts, wide, hidden)
    incoming_one = contract(grad_linear_two, second_low, 1, 1)
    sums_one, (returned,) = total(
        [jnp.sum(incoming_one * unit_one, 0), jnp.sum(incoming_one, 0)],
        None,
        [replies],
        (("ids", True),),
        3,
    )
    outgoing_one = norm_back(
        incoming_one, unit_one, norm_all[0], scale_one, live_mask, sums_one[0], sums_one[1], live_count
    )
    grad_linear_one = (mish_slope(linear_one) * outgoing_one).astype(jnp.bfloat16)
    local_first = contract(features, grad_linear_one, 0, 0)
    tokens_mine = lax.dynamic_slice(token_slots, (part * token_piece,), (token_piece,))
    second_sum, final_sum, first_sum, tokens = reduce_grads(
        (local_second, local_final, local_first),
        (
            (wide, hidden, 8, True, jnp.bfloat16),
            (wide, local_final.shape[2], 1, True, jnp.float32),
            (features.shape[1], wide, 2, False, jnp.bfloat16),
        ),
        returned,
        tokens_mine.reshape(1, token_piece),
        4,
    )
    token_embed = tokens.transpose(0, 2, 1).reshape(token_count, out_width)
    grad_second = second_sum[:width].reshape(width, parts, wide)
    grad_second = grad_second[:, :, :width].reshape(width, parts * width).T
    grad_final = final_sum[:width, :out_width]
    grad_first = first_sum[:, :width]
    start = part * wide
    grad_norm = lax.dynamic_slice(jnp.stack([*sums_one, *sums_two]), (0, start), (4, width))
    momentum_first, variance_first, master_first = adam(
        weight_first, moment_first, square_first, grad_first, rate_matrix, decay_matrix
    )
    momentum_second, variance_second, master_second = adam(
        weight_second, moment_second, square_second, grad_second, rate_matrix, decay_matrix
    )
    momentum_final, variance_final, master_final = adam(
        weight_final, moment_final, square_final, grad_final, rate_matrix, decay_matrix
    )
    momentum_norm, variance_norm, master_norm = adam(
        norm_params, moment_norm, square_norm, grad_norm, rate_norm, 0.0
    )
    momentum_bias, variance_bias, master_bias = adam(
        bias_final, moment_bias, square_bias, grad_bias, rate_bias, 0.0
    )
    return (
        token_embed,
        momentum_first,
        variance_first,
        master_first,
        master_first.astype(jnp.bfloat16),
        momentum_second,
        variance_second,
        master_second,
        master_second.astype(jnp.bfloat16),
        momentum_final,
        variance_final,
        master_final,
        master_final.astype(jnp.bfloat16),
        momentum_norm,
        variance_norm,
        master_norm,
        momentum_bias,
        variance_bias,
        master_bias,
    )


def solution(mesh):
    rows = P("ids", None)
    grid = P("ids", "mdl")
    columns = P(None, "mdl")
    mdl_rows = P("mdl", None)
    return jax.shard_map(
        body,
        mesh=mesh,
        in_specs=(grid, rows, P("ids"), P("ids"), rows, grid, columns, mdl_rows, columns, P())
        + (grid,) * 2
        + (columns,) * 2
        + (mdl_rows,) * 2
        + (columns,) * 2
        + (P(),) * 2,
        out_specs=(rows,)
        + (grid,) * 4
        + (columns,) * 4
        + (mdl_rows,) * 4
        + (columns,) * 3
        + (P(),) * 3,
        check_vma=False,
    )
```

time: 1010 us -> 488 us (0.48)
  waiting for transfers between devices: 477 us -> 0.04 us
  blocking collectives: 262 us -> 0 us
  Pallas kernels: 0 us -> 253 us
  other arithmetic: 72.2 us -> 44.6 us
  starting transfers between devices: 15 us -> 0.04 us
    psum x2 -> x0, waiting for transfers between devices: 264 us -> none  [the longest x1 155 us: body(): grad_second = lax.psum(grad_second, 'ids')]
    pallas_call x0 -> x6, Pallas kernels: none -> 253 us  [the longest x1 144 us: reduce_grads(): pl.pallas_call(functools.partial(reduce_kernel, parts, owners, plan), out...]
    reduce_scatter x3 -> x0, waiting for transfers between devices: 205 us -> none  [the longest x1 127 us: body(): lax.psum_scatter(local_second, 'mdl', scatter_dimension=0, tiled=False)]
    psum x4 -> x0, blocking collectives: 160 us -> none  [the longest x1 40.7 us: body(): lax.psum((jnp.stack([jnp.sum(incoming_one * unit_one, 0), jnp.sum(incomin...]
    all_gather x5 -> x0, blocking collectives: 83.5 us -> none  [the longest x1 48.9 us: body(): lax.all_gather(jnp.pad(norm_params, ((0, 0), (0, more))), 'mdl', axis=1,...]
    dot_general x5 -> x1, matrix products: 45.3 us -> 6.82 us  [body(): row_part = jnp.dot(arrived, pick_rows, preferred_element_type=jnp.float32)]
    dot_general x11 -> x8, matrix products: 45.5 us -> 81.2 us  [contract(): lax.dot_general(left, right, (((left_dim,), (right_dim,)), ((), ())), pre...]
    convert_element_type x4 -> x1, other arithmetic: 19.6 us -> 0.96 us  [body(): weight_first.astype(jnp.bfloat16)]
  transfers between devices with their start and end apart: 12 -> 1, of which waited for: 7 -> 0; matrix products, arithmetic and copies ran while one was open for 12% -> 9% of each run, Pallas kernels for 0% -> 3%
where the time goes in v2:
time: 488 us; the launch traced here: 479 us
  Pallas kernels  253 us (52%)
  matrix products  120 us (25%)
  local copies, waits for them, and re-layouts  46.7 us (10%)
  other arithmetic  44.6 us (9%)
  between operations  15.6 us (3%)
    pallas_call x1, Pallas kernels, reduce_grads(): pl.pallas_call(functools.partial(reduce_kernel, parts, owners, plan), out...  144 us
    dot_general x8, matrix products, contract(): lax.dot_general(left, right, (((left_dim,), (right_dim,)), ((), ())), pre...  81.2 us
    pallas_call x1, Pallas kernels, front(): pl.pallas_call(functools.partial(front_kernel, parts, owners), out_shape=...  57.2 us
    pallas_call x4, Pallas kernels, exchange(): pl.pallas_call(functools.partial(exchange_kernel, parts, owners, kinds),...  51.9 us
    dot_general x1, matrix products, body(): jnp.dot(normed_one, second_low, preferred_element_type=jnp.float32)  22 us
    convert_element_type x1, other arithmetic, body(): (mish_slope(linear_two) * outgoing_two).astype(jnp.bfloat16)  11.4 us
    unnamed x71, local copies, waits for them, and re-layouts  11.2 us
  transfers between devices with their start and end apart: 1, of which 0 were waited for; matrix products, arithmetic and copies ran while one was open for 9% of the time, Pallas kernels for 3%

profile of v2, /device:TPU:0, one launch (start us, length us, event | category | flops | bytes accessed | tf_op | source)
XLA Modules:
  0.0 479.3 jit_solution(9519803941303940085)
XLA Ops:
  7.3 2.8 add_convert_fusion.2
  10.1 1.0 convert_element_type.76
  11.2 0.8 subtract_select_fusion
  12.1 0.8 convert_bitcast_fusion
  13.0 3.4 convert_element_type.80
  16.4 6.3 %reshape.203 = bf16[4,450,450]{1,0,2:T(4,128)(2,1)} reshape(bf16[1800,450]{0,1:T(8,128)(2,1)} %convert_element_type.80) | data formatting | bytes 3240000 | tf_op jit(solution)/shard_map/reshape | solution.py:622
  22.7 2.3 pad.31
  25.0 1.9 copy.113
  27.0 57.2 %front.1 = (bf16[1024,2048]{1,0:T(8,128)(2,1)S(1)}, bf16[1024,1024]{1,0:T(8,128)(2,1)S(1)}, f32[4,8,512]{2,1,0:T(8,128)S(1)}, bf16[4,32,512]{2,1,0:T(8,128)(2,1)S(1)}, s32[8,1,1024]{2,1,0:T(1,128)S(1)}) custom-call(bf16[128,512]{1,0:T(8,128)(2,1)S(1)} %pad.28.first, bf16[4,1024,256]{2,1,0:T(8,128)(2,1)S(1)} %bitcast.128, f32[8,512]{1,0:T(8,128)S(1)} %pad.29.norms, ...), custom_call_target="tpu_custom_call" | custom-call | tf_op jit(solution)/shard_map/front/pallas_call | solution.py:262
  84.2 1.9 copy-done.2
  86.2 1.3 copy-done.4
  87.5 0.8 copy.98
  88.4 3.4 convert_reduce_fusion
  92.5 13.2 %subtract_convert_fusion = (bf16[32,2048]{1,0:T(8,128)(2,1)S(1)}, bf16[32,2048]{1,0:T(8,128)(2,1)S(1)}) fusion(bf16[8192,32]{0,1:T(8,128)(2,1)S(1)} %copy-done, s32[8192]{0:T(1024)S(1)} %fusion.26), kind=kOutput, calls=%fused_computation.50 | convolution fusion | flops 1090846720 | bytes 819200 | tf_op jit(solution)/shard_map/dot_general | solution.py:41
  106.4 9.5 %multiply_reduce_fusion.1 = (f32[2048]{0:T(1024)S(1)}, f32[2048]{0:T(1024)S(1)}, f32[1024,2048]{1,0:T(8,128)}) fusion(f32[1024]{0:T(1024)S(1)} %convert_reduce_fusion, bf16[1024,1024]{1,0:T(8,128)(2,1)S(1)} %copy-done.5, bf16[1024,2048]{1,0:T(8,128)(2,1)S(1)} %copy-done.3), kind=kOutput, calls=%fused_computation.14 | convolution fusion | flops 4318031872 | bytes 14700544 | tf_op jit(solution)/shard_map/dot_general | solution.py:647
  116.0 1.3 select_maximum_fusion.1.refs_0_
  117.3 15.3 %exchange.4 = (f32[40,128]{1,0:T(8,128)}, bf16[8,64,256]{2,1,0:T(8,128)(2,1)}) custom-call(f32[40,128]{1,0:T(8,128)} %select_maximum_fusion.1.refs_0_, bf16[8,64,256]{2,1,0:T(8,128)(2,1)} %bitcast.140), custom_call_target="tpu_custom_call" | custom-call | tf_op jit(solution)/shard_map/exchange/pallas_call | solution.py:160
  132.6 1.3 slice.74
  133.8 1.0 copy.109
  134.8 6.8 %fusion.2 = f32[64,4096]{1,0:T(8,128)S(1)} fusion(bf16[64,2048]{1,0:T(8,128)(2,1)S(1)} %bitcast.148, s32[2048]{0:T(1024)S(1)} %bitcast.163), kind=kOutput, calls=%fused_computation.4 | convolution fusion | flops 1082130432 | bytes 1318912 | tf_op jit(solution)/shard_map/dot_general | solution.py:663
  141.7 0.8 copy.117
  143.2 0.9 copy.95
  144.0 0.8 copy.96
  147.0 22.0 %multiply_reduce_fusion = (f32[2048]{0:T(1024)S(1)}, f32[2048]{0:T(1024)S(1)}, f32[1024,2048]{1,0:T(8,128)}, f32[1024,2048]{1,0:T(8,128)}) fusion(f32[1024]{0:T(1024)S(1)} %convert_reduce_fusion, bf16[2048,2048]{0,1:T(8,128)(2,1)} %all-gather.2.cloned.1.call-done, f32[2048]{0:T(1024)S(1)} %bitcast.174, f32[2048]{0:T(1024)S(1)} %fusion.36, ...), kind=kOutput, calls=%fused_computation.12 | convolution fusion | flops 8638164992 | bytes 33607680 | tf_op jit(solution)/shard_map/dot_general | solution.py:665
  169.6 11.3 %exchange.5 = (f32[32,128]{1,0:T(8,128)}, f32[4,32,1024]{2,1,0:T(8,128)}) custom-call(f32[32,128]{1,0:T(8,128)} %pad_maximum_fusion.1.refs_0_, f32[4,32,1024]{2,1,0:T(8,128)} %bitcast.138), custom_call_target="tpu_custom_call" | custom-call | tf_op jit(solution)/shard_map/exchange/pallas_call | solution.py:160
  180.9 1.4 fusion.34
  182.3 1.4 divide_bitcast_fusion
  183.6 1.1 reduce_sum.104
  184.7 5.8 %convert_reduce_fusion.1 = (f32[32]{0:T(128)S(1)}, bf16[32,1024]{1,0:T(8,128)(2,1)S(1)}, bf16[32,1024]{1,0:T(8,128)(2,1)}) fusion(f32[32,1024]{1,0:T(8,128)S(1)} %reduce_sum.104, f32[1024]{0:T(1024)S(1)} %broadcast_multiply_fusion, f32[32]{0:T(128)S(1)} %copy-done.26, bf16[32,2048]{1,0:T(8,128)(2,1)S(1)} %bitcast.142, f32[1024,2048]{1,0:T(8,128)} %get-tuple-element.161, ...), kind=kOutput, calls=%fused_computation.52 | convolution fusion | flops 144932832 | bytes 8818944 | tf_op jit(solution)/shard_map/dot_general | solution.py:41
  190.5 4.2 multiply_reduce_fusion.3
  194.7 2.5 fusion.21
  197.8 13.5 %exchange.6 = (f32[40,128]{1,0:T(8,128)}, bf16[4,32,1024]{2,1,0:T(8,128)(2,1)}) custom-call(f32[40,128]{1,0:T(8,128)} %select_maximum_fusion.refs_0_, bf16[32,1024]{1,0:T(8,128)(2,1)} %get-tuple-element.164.refs_1_), custom_call_target="tpu_custom_call" | custom-call | tf_op jit(solution)/shard_map/exchange/pallas_call | solution.py:160
  211.4 0.9 fusion.58
  212.2 1.1 copy.111
  213.3 7.0 %fusion.17 = bf16[32,2048]{1,0:T(8,128)(2,1)S(1)} fusion(bf16[32,4096]{1,0:T(8,128)(2,1)S(1)} %bitcast.150, s32[2048]{0:T(1024)S(1)} %bitcast.164), kind=kOutput, calls=%fused_computation.40 | convolution fusion | flops 545325056 | bytes 401408 | tf_op jit(solution)/shard_map/dot_general | solution.py:41
  221.0 11.4 %multiply_convert_fusion.1 = bf16[1024,2048]{1,0:T(8,128)(2,1)S(1)} fusion(f32[1024,2048]{1,0:T(8,128)S(1)} %copy-done.7, f32[1024,2048]{1,0:T(8,128)} %get-tuple-element.178, f32[1024,2048]{1,0:T(8,128)} %get-tuple-element.161, f32[]{:T(128)} %bitcast.10, f32[2048]{0:T(1024)S(1)} %get-tuple-element.170, f32[2048]{0:T(1024)S(1)} %get-tuple-element.171, ...), kind=kLoop, calls=%fused_computation.19 | loop fusion | flops 52428800 | bytes 29405188 | tf_op jit(solution)/shard_map/convert_element_type | solution.py:703
  232.5 15.7 %fusion.19 = f32[2048,2048]{1,0:T(8,128)} fusion(bf16[1024,2048]{1,0:T(8,128)(2,1)S(1)} %multiply_convert_fusion.1, f32[2048]{0:T(1024)S(1)} %bitcast.175, f32[2048]{0:T(1024)S(1)} %fusion.36, f32[2048]{0:T(1024)S(1)} %divide_bitcast_fusion.1, f32[2048]{0:T(1024)S(1)} %bitcast.172, f32[1024,2048]{1,0:T(8,128)} %get-tuple-element.177), kind=kOutput, calls=%fused_computation.55 | convolution fusion | flops 8615100416 | bytes 29392896 | tf_op jit(solution)/shard_map/dot_general | solution.py:41
  248.1 15.4 %multiply_reduce_fusion.2 = (f32[2048]{0:T(1024)S(1)}, f32[2048]{0:T(1024)S(1)}, f32[1024,2048]{1,0:T(8,128)}) fusion(f32[2048]{0:T(1024)S(1)} %fusion.36, f32[2048]{0:T(1024)S(1)} %divide_bitcast_fusion.1, f32[1024,2048]{1,0:T(8,128)} %get-tuple-element.177, bf16[1024,2048]{1,0:T(8,128)(2,1)S(1)} %multiply_convert_fusion.1, ...), kind=kOutput, calls=%fused_computation.18 | convolution fusion | flops 8615096320 | bytes 29392896 | tf_op jit(solution)/shard_map/dot_general | solution.py:41
  264.1 11.8 %exchange.7 = (f32[32,128]{1,0:T(8,128)}, bf16[8,32,256]{2,1,0:T(8,128)(2,1)}) custom-call(f32[32,128]{1,0:T(8,128)} %pad_maximum_fusion.2.refs_0_, bf16[8,32,256]{2,1,0:T(8,128)(2,1)} %bitcast.146), custom_call_target="tpu_custom_call" | custom-call | tf_op jit(solution)/shard_map/exchange/pallas_call | solution.py:160
  276.7 2.3 pad.34.refs_1_
  279.0 17.4 %fusion.12.refs_2_ = f32[1024,2048]{1,0:T(8,128)} fusion(bf16[1024,1024]{1,0:T(8,128)(2,1)S(1)} %copy-done.5, f32[1024,2048]{1,0:T(8,128)} %get-tuple-element.181, f32[1024,2048]{1,0:T(8,128)} %get-tuple-element.177, f32[2048]{0:T(1024)S(1)} %get-tuple-element.175, f32[2048]{0:T(1024)S(1)} %get-tuple-element.174, f32[]{:T(128)} %bitcast.10, ...), kind=kOutput, calls=%fused_computation.33 | convolution fusion | flops 4349493248 | bytes 27308036 | tf_op jit(solution)/shard_map/dot_general | solution.py:41
  296.4 143.5 %reduce_grads.1 = (f32[4,2,64,2048]{3,2,1,0:T(8,128)}, f32[4,2,64,128]{3,2,1,0:T(8,128)}, f32[128,512]{1,0:T(8,128)}, bf16[4,32,2048]{2,1,0:T(8,128)(2,1)}) custom-call(f32[4,512,2048]{2,1,0:T(8,128)} %bitcast.132, f32[4,512,128]{2,1,0:T(8,128)} %pad.34.refs_1_, f32[1024,2048]{1,0:T(8,128)} %fusion.12.refs_2_, ...), custom_call_target="tpu_custom_call" | custom-call | tf_op jit(solution)/shard_map/reduce_grads/pallas_call | solution.py:536
  439.9 4.3 slice.98
  444.3 5.6 %reshape.225 = f32[450,4,512]{2,1,0:T(4,128)} reshape(f32[450,2048]{1,0:T(8,128)} %slice.98) | data formatting | bytes 7372800 | tf_op jit(solution)/shard_map/reshape | solution.py:731
  449.9 5.7 %reshape.226 = f32[450,1800]{1,0:T(8,128)} reshape(f32[450,4,450]{2,1,0:T(4,128)} %bitcast.133) | data formatting | bytes 6480000 | tf_op jit(solution)/shard_map/reshape | solution.py:732
  459.3 0.9 copy.112
  460.1 1.3 multiply_subtract_fusion.4
  461.5 9.1 %fusion.51 = (bf16[1800,450]{0,1:T(8,128)(2,1)}, f32[1800,450]{0,1:T(8,128)}, f32[1800,450]{0,1:T(8,128)}, f32[1800,450]{0,1:T(8,128)}) fusion(f32[1800,450]{0,1:T(8,128)} %param.26, f32[450,1800]{1,0:T(8,128)} %reshape.226, f32[1800,450]{0,1:T(8,128)} %param.33, f32[1800,450]{0,1:T(8,128)} %param.32), kind=kLoop, calls=%fused_computation.118 | loop fusion | flops 12960000 | bytes 24300000 | tf_op jit(solution)/shard_map/convert_element_type | solution.py:761
  (97 shorter events, 12.0 us)
Async XLA Ops:
  7.2 85.3 %copy-start = (bf16[8192,32]{0,1:T(8,128)(2,1)S(1)}, bf16[8192,32]{0,1:T(8,128)(2,1)}, u32[]{:S(2)}) copy-start(bf16[8192,32]{0,1:T(8,128)(2,1)} %param.24) | copy-start | bytes 1572868
  7.2 139.7 %all-gather.2.cloned.1.call-start = ((), (), s32[]{:S(2)}) async-start(), calls=%async_computation | async-start | bytes 10485760 | tf_op jit(solution)/shard_map/all_gather | solution.py:626
  13.0 14.0 %copy-start.21 = (f32[4,450]{1,0:T(4,128)S(1)}, f32[4,450]{1,0:T(4,128)}, u32[]{:S(2)}) copy-start(f32[4,450]{1,0:T(4,128)} %param.28) | copy-start | bytes 21604
  16.4 71.2 %copy-start.11 = (f32[128,450]{0,1:T(8,128)S(1)}, f32[128,450]{0,1:T(8,128)}, u32[]{:S(2)}) copy-start(f32[128,450]{0,1:T(8,128)} %param.25) | copy-start | bytes 691204
  16.4 76.0 %copy-start.20 = (s32[8192]{0:T(1024)S(1)}, s32[8192]{0:T(1024)}, u32[]{:S(2)}) copy-start(s32[8192]{0:T(1024)} %param.23) | copy-start | bytes 98308
  84.2 1.9 copy-start.2
  86.2 1.3 copy-start.4
  92.5 14.0 %copy-start.3 = (bf16[1024,2048]{1,0:T(8,128)(2,1)S(1)}, bf16[1024,2048]{1,0:T(8,128)(2,1)}, u32[]{:S(2)}) copy-start(bf16[1024,2048]{1,0:T(8,128)(2,1)} %copy-done.2) | copy-start | bytes 12582916
  92.5 14.0 %copy-start.5 = (bf16[1024,1024]{1,0:T(8,128)(2,1)S(1)}, bf16[1024,1024]{1,0:T(8,128)(2,1)}, u32[]{:S(2)}) copy-start(bf16[1024,1024]{1,0:T(8,128)(2,1)} %copy-done.4) | copy-start | bytes 6291460
  116.0 27.2 %copy-start.15 = (f32[128,450]{0,1:T(8,128)S(1)}, f32[128,450]{0,1:T(8,128)}, u32[]{:S(2)}) copy-start(f32[128,450]{0,1:T(8,128)} %param.30) | copy-start | bytes 691204
  116.0 28.1 %copy-start.16 = (f32[128,450]{0,1:T(8,128)S(1)}, f32[128,450]{0,1:T(8,128)}, u32[]{:S(2)}) copy-start(f32[128,450]{0,1:T(8,128)} %param.31) | copy-start | bytes 691204
  132.6 13.0 %copy-start.23 = (f32[40,128]{1,0:T(8,128)S(1)}, f32[40,128]{1,0:T(8,128)}, u32[]{:S(2)}) copy-start(f32[40,128]{1,0:T(8,128)} %get-tuple-element.43) | copy-start | bytes 61444
  147.0 37.8 %copy-start.26 = (f32[32]{0:T(128)S(1)}, f32[32]{0:T(128)}, u32[]{:S(2)}) copy-start(f32[32]{0:T(128)} %param.29) | copy-start | bytes 388
  184.7 5.8 %copy-start.6 = (f32[1024,2048]{1,0:T(8,128)S(1)}, f32[1024,2048]{1,0:T(8,128)}, u32[]{:S(2)}) copy-start(f32[1024,2048]{1,0:T(8,128)} %get-tuple-element.161) | copy-start | bytes 25165828
  211.3 9.7 %copy-start.7 = (f32[1024,2048]{1,0:T(8,128)S(1)}, f32[1024,2048]{1,0:T(8,128)}, u32[]{:S(2)}) copy-start(f32[1024,2048]{1,0:T(8,128)} %get-tuple-element.180) | copy-start | bytes 25165828
  221.0 27.1 %slice-start = ((s8[8388608]{0:T(1024)(128)(4,1)}), s8[4194304]{0:T(1024)(128)(4,1)S(1)}, s32[]{:S(2)}) async-start(s8[8388608]{0:T(1024)(128)(4,1)} %bitcast.179), calls=%async_computation.1 | async-start | bytes 8388608
  232.4 15.7 %slice-start.1 = ((s8[8388608]{0:T(1024)(128)(4,1)}), s8[4194304]{0:T(1024)(128)(4,1)S(1)}, s32[]{:S(2)}) async-start(s8[8388608]{0:T(1024)(128)(4,1)} %bitcast.179), calls=%async_computation.2 | async-start | bytes 8388608
  444.3 11.4 %copy-start.8 = (f32[128,450]{1,0:T(8,128)S(1)}, f32[128,450]{1,0:T(8,128)}, u32[]{:S(2)}) copy-start(f32[128,450]{1,0:T(8,128)} %copy.98) | copy-start | bytes 691204
  444.3 11.4 %copy-start.9 = (f32[128,450]{1,0:T(8,128)S(1)}, f32[128,450]{1,0:T(8,128)}, u32[]{:S(2)}) copy-start(f32[128,450]{1,0:T(8,128)} %copy.95) | copy-start | bytes 691204
  444.3 11.4 %copy-start.10 = (f32[128,450]{1,0:T(8,128)S(1)}, f32[128,450]{1,0:T(8,128)}, u32[]{:S(2)}) copy-start(f32[128,450]{1,0:T(8,128)} %copy.96) | copy-start | bytes 691204
  444.3 11.4 %copy-start.13 = (f32[128,512]{1,0:T(8,128)S(1)}, f32[128,512]{1,0:T(8,128)}, u32[]{:S(2)}) copy-start(f32[128,512]{1,0:T(8,128)} %get-tuple-element.54) | copy-start | bytes 786436
  444.3 14.9 %copy-start.17 = (f32[4,2,64,128]{3,2,1,0:T(8,128)S(1)}, f32[4,2,64,128]{3,2,1,0:T(8,128)}, u32[]{:S(2)}) copy-start(f32[4,2,64,128]{3,2,1,0:T(8,128)} %get-tuple-element.56) | copy-start | bytes 786436
  444.3 15.0 %copy-start.12 = (bf16[4,32,2048]{2,1,0:T(8,128)(2,1)S(1)}, bf16[4,32,2048]{2,1,0:T(8,128)(2,1)}, u32[]{:S(2)}) copy-start(bf16[4,32,2048]{2,1,0:T(8,128)(2,1)} %get-tuple-element.53) | copy-start | bytes 1572868
  444.3 15.9 %copy-start.27 = (f32[32]{0:T(128)S(1)}, f32[32]{0:T(128)}, u32[]{:S(2)}) copy-start(f32[32]{0:T(128)} %param.39) | copy-start | bytes 388
  444.3 15.8 %copy-start.28 = (f32[32]{0:T(128)S(1)}, f32[32]{0:T(128)}, u32[]{:S(2)}) copy-start(f32[32]{0:T(128)} %param.38) | copy-start | bytes 388
  460.1 11.8 %copy-start.1 = (bf16[8192,32]{0,1:T(8,128)(2,1)S(1)}, bf16[8192,32]{0,1:T(8,128)(2,1)}, u32[]{:S(2)}) copy-start(bf16[8192,32]{0,1:T(8,128)(2,1)} %param.24) | copy-start | bytes 1572868
  461.4 9.1 %copy-start.14 = (f32[450,32]{0,1:T(8,128)S(1)}, f32[450,32]{0,1:T(8,128)}, u32[]{:S(2)}) copy-start(f32[450,32]{0,1:T(8,128)} %param.27) | copy-start | bytes 172804
  461.4 9.1 %copy-start.18 = (f32[450,32]{0,1:T(8,128)S(1)}, f32[450,32]{0,1:T(8,128)}, u32[]{:S(2)}) copy-start(f32[450,32]{0,1:T(8,128)} %param.35) | copy-start | bytes 172804
  461.4 9.1 %copy-start.19 = (f32[450,32]{0,1:T(8,128)S(1)}, f32[450,32]{0,1:T(8,128)}, u32[]{:S(2)}) copy-start(f32[450,32]{0,1:T(8,128)} %param.34) | copy-start | bytes 172804
  461.4 9.8 %copy-start.22 = (f32[4,450]{1,0:T(4,128)S(1)}, f32[4,450]{1,0:T(4,128)}, u32[]{:S(2)}) copy-start(f32[4,450]{1,0:T(4,128)} %param.28) | copy-start | bytes 21604
  461.4 9.8 %copy-start.24 = (f32[4,450]{1,0:T(4,128)S(1)}, f32[4,450]{1,0:T(4,128)}, u32[]{:S(2)}) copy-start(f32[4,450]{1,0:T(4,128)} %param.37) | copy-start | bytes 21604
  461.5 9.8 %copy-start.25 = (f32[4,450]{1,0:T(4,128)S(1)}, f32[4,450]{1,0:T(4,128)}, u32[]{:S(2)}) copy-start(f32[4,450]{1,0:T(4,128)} %param.36) | copy-start | bytes 21604
Sparse Core Ops, SparseCore 0:
  87.6 56.9 all-gather.1

commit v3 on v2

--- a/solution.py
+++ b/solution.py
@@ -73,7 +73,6 @@
 
 
 MESH = pl.DeviceIdType.MESH
-BIG = 60 * 1024 * 1024
 
 
 def greet(peers):
@@ -315,14 +314,21 @@
     pass
 
 
-def reduce_kernel(parts, owners, plan, *refs):
+BLOCK = 256
+
+
+def back_kernel(parts, owners, plan, *refs):
     half = parts // 2
     count = len(plan)
-    inputs, (replies, picks) = refs[:count], refs[count : count + 2]
-    outputs, tokens_out = refs[count + 2 : 2 * count + 2], refs[2 * count + 2]
-    scratch = list(refs[2 * count + 3 :])
+    given = refs[: count - 1]
+    slopes, weights, turned, linear, vectors, ratio, replies, picks = refs[count - 1 : count + 7]
+    outputs, tokens_out, sums_out = refs[count + 7 : 2 * count + 7], refs[2 * count + 7], refs[2 * count + 8]
+    scratch = list(refs[2 * count + 9 :])
     gathered, made, sp, rp, st_, rt_ = scratch[:6]
-    scratch = scratch[6:]
+    ra, rb = scratch[18:20]
+    held, stream, stream_sem, grown, gains, shifts, near, far, sn, rn, sf_, rf_ = scratch[6:18]
+    scratch = scratch[20:]
+    inputs = given + (held,)
     part = lax.axis_index("mdl")
     owner = lax.axis_index("ids")
     low, place = lax.rem(part, 2), part // 2
@@ -341,48 +347,64 @@
             u.piece = rows // owners
             u.cols = pl.ds(c * u.width, u.width)
             u.source, u.out = inputs[n], outputs[n]
+            u.here = n == count - 1
+            u.after = None
             units.append(u)
+    for u, v in zip(units, units[2:]):
+        if u.own is v.own and u.own is not None:
+            u.after = v
     greet([gap("mdl", parts, d) for d in range(1, parts)] + [gap("ids", owners, d) for d in range(1, owners)])
 
     def taken(u, k):
-        if len(u.source.shape) == 3:
+        if not u.here:
             return u.source.at[k, :, u.cols]
         start = pl.multiple_of(k * u.lanes + u.c * u.width, u.width)
         return u.source.at[:, pl.ds(start, u.width)]
 
+    def fetch(u):
+        u.mine = [
+            pltpu.make_async_copy(taken(u, low + 2 * i), u.own.at[u.c % 2, i], u.sl.at[u.c, i])
+            for i in range(half)
+        ]
+        for copy in u.mine:
+            copy.start()
+
     def begin(u):
-        u.first, u.mine = [], []
-        for i in range(half):
-            u.first.append(
-                push(
-                    taken(u, 1 - low + 2 * i),
-                    u.got.at[i, :, u.cols],
-                    u.s0.at[u.c, i],
-                    u.r0.at[u.c, i],
-                    pair,
-                )
+        u.first = [
+            push(
+                taken(u, 1 - low + 2 * i),
+                u.got.at[i, :, u.cols],
+                u.s0.at[u.c, i],
+                u.r0.at[u.c, i],
+                pair,
             )
-            u.mine.append(
-                pltpu.make_async_copy(
-                    taken(u, low + 2 * i), u.own.at[i, :, u.cols], u.sl.at[u.c, i]
-                )
-            )
-        for copy in u.first + u.mine:
+            for i in range(half)
+        ]
+        for copy in u.first:
             copy.start()
 
     def sweep(u, body):
         step = min(u.rows, 64)
-        blocks(u.rows, step, lambda k: body((pl.ds(k, step), u.cols)))
+        blocks(u.rows, step, lambda k: body(pl.ds(k, step)))
+
+    def own_part(u, i, at):
+        if u.here:
+            start = pl.multiple_of((low + 2 * i) * u.lanes + u.c * u.width, u.width)
+            return u.source[at, pl.ds(start, u.width)]
+        return u.own[u.c % 2, i, at]
 
     def to_cross(u):
-        for copy in u.first + u.mine:
+        for copy in u.first + ([] if u.here else u.mine):
             copy.wait()
 
         def body(at):
-            spot = (1 - place,) + at
-            u.out_y[at] = (u.own[spot] + u.got[spot]).astype(u.wire)
+            away = own_part(u, 1 - place, at) + u.got[1 - place, at, u.cols]
+            u.out_y[at, u.cols] = away.astype(u.wire)
+            u.got[place, at, u.cols] = own_part(u, place, at) + u.got[place, at, u.cols]
 
         sweep(u, body)
+        if u.after is not None:
+            fetch(u.after)
         u.second = push(
             u.out_y.at[:, u.cols], u.in_y.at[:, u.cols], u.sy.at[u.c], u.ry.at[u.c], cross
         )
@@ -392,10 +414,9 @@
         u.second.wait()
 
         def body(at):
-            spot = (place,) + at
-            value = u.own[spot] + u.got[spot] + u.in_y[at].astype(jnp.float32)
-            u.own[spot] = value
-            u.out_f[at] = value.astype(u.wire)
+            value = u.got[place, at, u.cols] + u.in_y[at, u.cols].astype(jnp.float32)
+            u.got[place, at, u.cols] = value
+            u.out_f[at, u.cols] = value.astype(u.wire)
 
         sweep(u, body)
         u.third = []
@@ -415,7 +436,7 @@
         for copy in u.third:
             copy.wait()
         here = pl.ds(pl.multiple_of(owner * u.piece, u.piece), u.piece)
-        value = u.own[place, here, u.cols]
+        value = u.got[place, here, u.cols]
         for d in range(1, owners):
             value = value + u.in_f[d, :, u.cols].astype(jnp.float32)
         if not u.keep:
@@ -448,6 +469,115 @@
         there = u.out.at[:, 1 - side, :, u.cols]
         push(there, there, u.st.at[u.c], u.rt.at[u.c], twin).wait_recv()
 
+    rows, hidden = slopes.shape
+    bands = hidden // BLOCK
+    step = 64
+
+    def band(k):
+        return pl.ds(pl.multiple_of(k * BLOCK, BLOCK), BLOCK)
+
+    def load(k, slot):
+        return pltpu.make_async_copy(linear.at[:, band(k)], stream.at[slot], stream_sem.at[slot])
+
+    def unit_rows(values, k):
+        mean, scale = vectors[0:1, band(k)], vectors[1:2, band(k)]
+        return (mish(values) - mean) * scale
+
+    def incoming(k, slot):
+        load(k, slot).wait()
+
+        def multiply(r):
+            at = pl.ds(r, rows // 2)
+            held[at, band(k)] = jnp.dot(
+                slopes[at, :], weights[:, band(k)], preferred_element_type=jnp.float32
+            )
+
+        blocks(rows, rows // 2, multiply)
+
+        def body(n, sums):
+            at = pl.ds(pl.multiple_of(n * step, step), step)
+            value = held[at, band(k)]
+            product = value * unit_rows(stream[slot, at, :], k)
+            return (
+                sums[0] + jnp.sum(product.reshape(step // 8, 8, BLOCK), 0),
+                sums[1] + jnp.sum(value.reshape(step // 8, 8, BLOCK), 0),
+            )
+
+        zero = jnp.zeros((8, BLOCK), jnp.float32)
+        gain, shift = lax.fori_loop(0, rows // step, body, (zero, zero))
+        gains[0:1, band(k)] = jnp.sum(gain, 0, keepdims=True)
+        shifts[0:1, band(k)] = jnp.sum(shift, 0, keepdims=True)
+
+    def outgoing(k, slot):
+        load(k, slot).wait()
+
+        def body(n, none):
+            at = pl.ds(pl.multiple_of(n * step, step), step)
+            values = stream[slot, at, :]
+            scale, gain = vectors[1:2, band(k)], vectors[2:3, band(k)]
+            pull = shifts[0:1, band(k)] + unit_rows(values, k) * gains[0:1, band(k)]
+            back = scale * (gain * held[at, band(k)] - ratio[at, :] * gain * pull)
+            grown[at, :] = (mish_slope(values) * back).astype(jnp.bfloat16)
+            return none
+
+        lax.fori_loop(0, rows // step, body, 0)
+
+        def multiply(r):
+            at = pl.ds(r, rows // 2)
+            held[at, band(k)] = jnp.dot(turned[at, :], grown[...], preferred_element_type=jnp.float32)
+
+        blocks(rows, rows // 2, multiply)
+
+    def bands_of(work, order):
+        def body(n, none):
+            for slot in range(2):
+                k = 2 * n + slot
+
+                @pl.when(k + 1 < bands)
+                def _():
+                    load(order(k + 1), 1 - slot).start()
+
+                work(order(k), slot)
+            return none
+
+        return body
+
+    def exchange_sums(meanwhile):
+        lines = hidden // 128
+        for n in range(lines):
+            at = slice(128 * n, 128 * (n + 1))
+            near[0, n : n + 1, :] = gains[0:1, at]
+            near[0, lines + n : lines + n + 1, :] = shifts[0:1, at]
+        copies = [
+            push(near.at[0], near.at[d], sn.at[d], rn.at[d], gap("mdl", parts, d))
+            for d in range(1, parts)
+        ]
+        for copy in copies:
+            copy.start()
+        meanwhile()
+        for copy in copies:
+            copy.wait()
+        total = near[part]
+        for k in range(1, parts):
+            total = total + near[lax.rem(part + parts - k, parts)]
+        far[0] = total
+        copies = [
+            push(far.at[0], far.at[d], sf_.at[d], rf_.at[d], gap("ids", owners, d))
+            for d in range(1, owners)
+        ]
+        for copy in copies:
+            copy.start()
+        for copy in copies:
+            copy.wait()
+        total = far[owner]
+        for k in range(1, owners):
+            total = total + far[lax.rem(owner + owners - k, owners)]
+        sums_out[...] = total
+        for n in range(lines):
+            at = slice(128 * n, 128 * (n + 1))
+            gains[0:1, at] = total[n : n + 1]
+            shifts[0:1, at] = total[lines + n : lines + n + 1]
+
     def share(source, target, send, recv):
         copies = [
             push(source, target.at[part], send.at[d], recv.at[d], gap("mdl", parts, d))
@@ -471,38 +601,94 @@
         summed = lax.fori_loop(0, owners, body, start)
         made[...] = summed.astype(jnp.bfloat16) if q == 0 else made[...] + summed.astype(jnp.bfloat16)
 
-    early = share(replies, gathered, sp, rp)
-    gathered[part] = replies[...]
-    for u in units:
+    asked = []
+    for d in range(1, owners):
+        peer = gap("ids", owners, d)
+        copy = push(replies.at[peer["ids"]], gathered.at[part, owner], ra.at[d], rb.at[d], peer)
+        copy.start()
+        asked.append(copy)
+    gathered[part, owner] = replies[owner]
+    whole = [u for u in units if not u.here]
+    own = [u for u in units if u.here]
+    for u in whole:
         begin(u)
+    for n, u in enumerate(whole):
+        if n == 0 or u.c < 2:
+            fetch(u)
+    plain = bands_of(incoming, lambda k: k)
+    load(0, 0).start()
+    per = bands // parts
+    spread = bands_of(outgoing, lambda k: lax.rem(k, parts) * per + k // parts)
     total = len(units)
-    late = []
     stages = (to_cross, to_owners, finish, to_twin, close)
-    for t in range(total + len(stages) - 1):
+    ready = [0]
+
+    def advance():
+        t = ready[0]
+        ready[0] += 1
         for s, stage in enumerate(stages):
             if 0 <= t - s < total:
                 stage(units[t - s])
-        if t == 0:
-            for copy in early:
-                copy.wait()
-        if t < parts:
-            select(t)
-        if t == parts - 1:
-            tokens_out[part] = made[...]
-            late = share(made, tokens_out, st_, rt_)
+
+    loops = bands // 2
+    lax.fori_loop(0, loops // 2, plain, 0)
+    advance()
+    lax.fori_loop(loops // 2, loops, plain, 0)
+    exchange_sums(advance)
+    advance()
+    for copy in asked:
+        copy.wait()
+    early = share(gathered.at[part], gathered, sp, rp)
+    load(0, 0).start()
+    for n in range(loops):
+        spread(n, 0)
+        if (n + 1) % (loops // per) == 0:
+            begin(own[(n + 1) * per // loops - 1])
+        advance()
+    for copy in early:
+        copy.wait()
+    for q in range(parts):
+        advance()
+        select(q)
+    tokens_out[part] = made[...]
+    late = share(made, tokens_out, st_, rt_)
+    while ready[0] < total + len(stages) - 1:
+        advance()
     for copy in late:
         copy.wait()
 
 
-def reduce_grads(arrays, plan, replies, picks, call):
+def back(arrays, plan, operands, replies, picks, call):
     parts, owners = lax.axis_size("mdl"), lax.axis_size("ids")
     half = parts // 2
+    slopes, weights, turned, linear, vectors, ratio = operands
+    size, hidden = slopes.shape
+    inputs = turned.shape[0]
+    assert inputs == size
     found_shape = (replies.shape[1], picks.shape[1])
+    dma = pltpu.SemaphoreType.DMA
+    lines = 2 * hidden // 128
     outs = []
     scratch = [
         pltpu.VMEM((parts,) + replies.shape, replies.dtype),
         pltpu.VMEM(found_shape, replies.dtype),
-    ] + [pltpu.SemaphoreType.DMA((parts,))] * 4
+    ] + [dma((parts,))] * 4
+    scratch += [
+        pltpu.VMEM((inputs, hidden), jnp.float32),
+        pltpu.VMEM((2, size, BLOCK), jnp.float32),
+        dma((2,)),
+        pltpu.VMEM((size, BLOCK), jnp.bfloat16),
+        pltpu.VMEM((8, hidden), jnp.float32),
+        pltpu.VMEM((8, hidden), jnp.float32),
+        pltpu.VMEM((parts, lines, 128), jnp.float32),
+        pltpu.VMEM((owners, lines, 128), jnp.float32),
+        dma((parts,)),
+        dma((parts,)),
+        dma((owners,)),
+        dma((owners,)),
+        dma((owners,)),
+        dma((owners,)),
+    ]
     for rows, lanes, chunks, keep, wire in plan:
         piece = rows // owners
         outs.append(
@@ -510,9 +696,8 @@
                 (owners // 2, 2, piece, lanes) if keep else (piece, lanes), jnp.float32
             )
         )
-        dma = pltpu.SemaphoreType.DMA
         scratch += [
-            pltpu.VMEM((half, rows, lanes), jnp.float32),
+            pltpu.VMEM((2, half, rows, lanes // chunks) if keep else (8, 128), jnp.float32),
             pltpu.VMEM((half, rows, lanes), jnp.float32),
             pltpu.VMEM((rows, lanes), wire),
             pltpu.VMEM((rows, lanes), wire),
@@ -533,19 +718,25 @@
                 dma((chunks,)),
                 dma((chunks,)),
             ]
+    held = pl.BlockSpec(memory_space=pl.ANY)
+    whole = pl.BlockSpec(memory_space=pltpu.VMEM)
     found = pl.pallas_call(
-        functools.partial(reduce_kernel, parts, owners, plan),
-        out_shape=tuple(outs) + (jax.ShapeDtypeStruct((parts,) + found_shape, replies.dtype),),
-        in_specs=[pl.BlockSpec(memory_space=pl.ANY)] * len(arrays)
-        + [pl.BlockSpec(memory_space=pltpu.VMEM)] * 2,
-        out_specs=(pl.BlockSpec(memory_space=pltpu.VMEM),) * (len(arrays) + 1),
+        functools.partial(back_kernel, parts, owners, plan),
+        out_shape=tuple(outs)
+        + (
+            jax.ShapeDtypeStruct((parts,) + found_shape, replies.dtype),
+            jax.ShapeDtypeStruct((lines, 128), jnp.float32),
+        ),
+        in_specs=[held] * len(arrays) + [whole, whole, whole, held, whole, whole] + [whole] * 2,
+        out_specs=(whole,) * (len(plan) + 2),
         scratch_shapes=scratch,
         compiler_params=pltpu.CompilerParams(
-            collective_id=call, has_side_effects=True, vmem_limit_bytes=BIG
+            collective_id=call, has_side_effects=True, vmem_limit_bytes=67043328
         ),
-        name="reduce_grads",
-    )(*arrays, replies, picks)
-    return tuple(v.reshape(-1, v.shape[-1]) for v in found[:-1]) + (found[-1],)
+        name="back",
+    )(*arrays, *operands, replies, picks)
+    grads = tuple(v.reshape(-1, v.shape[-1]) for v in found[: len(plan)])
+    return grads + (found[-2], found[-1].reshape(2, hidden))
 
 
 def total(vectors, small, extras, kinds, call):
@@ -619,11 +810,11 @@
     norm_all = norm_all.transpose(1, 0, 2).reshape(-1, hidden)[:4]
     final_low = final_all.transpose(1, 0, 2).reshape(out_width, hidden)
     second_part = jnp.pad(
-        weight_second.astype(jnp.bfloat16).reshape(parts, width, width),
-        ((0, 0), (0, more), (0, more)),
-    ).reshape(hidden, wide)
+        weight_second.T.astype(jnp.bfloat16).reshape(width, parts, width),
+        ((0, more), (0, 0), (0, more)),
+    ).reshape(wide, hidden)
     second_part, first_low = lax.optimization_barrier((second_part, first_low))
-    second_low = lax.all_gather(second_part, "mdl", axis=1, tiled=True)
+    second_low = lax.all_gather(second_part, "mdl", axis=0, tiled=True)
 
     received = received.reshape(owners, slots_per)
     here = part * rows + jnp.arange(rows, dtype=jnp.int32)
@@ -662,7 +853,7 @@
     arrived = arrived.transpose(1, 0, 2).reshape(2 * out_width, owners * piece)
     row_part = jnp.dot(arrived, pick_rows, preferred_element_type=jnp.float32)
     row_part = (row_part[:out_width] + row_part[out_width:]).reshape(out_width, parts, rows)
-    linear_two = jnp.dot(normed_one, second_low, preferred_element_type=jnp.float32)
+    linear_two = contract(normed_one, second_low, 1, 1)
     active_two = mish(linear_two)
     weighted_two = live_mask[:, None] * active_two
     sums_two, (row_parts,) = total(
@@ -702,28 +893,23 @@
     )
     grad_linear_two = (mish_slope(linear_two) * outgoing_two).astype(jnp.bfloat16)
     local_second = contract(grad_linear_two, normed_one, 0, 0).reshape(parts, wide, hidden)
-    incoming_one = contract(grad_linear_two, second_low, 1, 1)
-    sums_one, (returned,) = total(
-        [jnp.sum(incoming_one * unit_one, 0), jnp.sum(incoming_one, 0)],
-        None,
-        [replies],
-        (("ids", True),),
-        3,
-    )
-    outgoing_one = norm_back(
-        incoming_one, unit_one, norm_all[0], scale_one, live_mask, sums_one[0], sums_one[1], live_count
-    )
-    grad_linear_one = (mish_slope(linear_one) * outgoing_one).astype(jnp.bfloat16)
-    local_first = contract(features, grad_linear_one, 0, 0)
     tokens_mine = lax.dynamic_slice(token_slots, (part * token_piece,), (token_piece,))
-    second_sum, final_sum, first_sum, tokens = reduce_grads(
-        (local_second, local_final, local_first),
+    second_sum, final_sum, first_sum, tokens, sums_one = back(
+        (local_second, local_final),
         (
             (wide, hidden, 8, True, jnp.bfloat16),
             (wide, local_final.shape[2], 1, True, jnp.float32),
-            (features.shape[1], wide, 2, False, jnp.bfloat16),
+            (features.shape[1], wide, wide // BLOCK, False, jnp.bfloat16),
         ),
-        returned,
+        (
+            grad_linear_two,
+            second_low,
+            features.T,
+            linear_one,
+            jnp.pad(jnp.stack([mean_one, scale_one, norm_all[0]]), ((0, 5), (0, 0))),
+            (live_mask / live_count)[:, None],
+        ),
+        replies,
         tokens_mine.reshape(1, token_piece),
         4,
     )

time: 488 us -> 465 us (0.953)
  matrix products: 120 us -> 87.8 us
  local copies, waits for them, and re-layouts: 46.7 us -> 52.1 us
    dot_general x1 -> x0, matrix products: 22 us -> none  [body(): jnp.dot(normed_one, second_low, preferred_element_type=jnp.float32)]
    pallas_call x1, Pallas kernels: 144 us -> 160 us  [back(): pl.pallas_call(functools.partial(back_kernel, parts, owners, plan), out_s...]
    dot_general x8 -> x7, matrix products: 81.2 us -> 67.9 us  [contract(): lax.dot_general(left, right, (((left_dim,), (right_dim,)), ((), ())), pre...]
    pallas_call x4 -> x3, Pallas kernels: 51.9 us -> 39.7 us  [exchange(): pl.pallas_call(functools.partial(exchange_kernel, parts, owners, kinds),...]
    unnamed x71 -> x67, local copies, waits for them, and re-layouts: 11.2 us -> 12.8 us
  transfers between devices with their start and end apart: 1 -> 1, of which waited for: 0 -> 0; matrix products, arithmetic and copies ran while one was open for 9% -> 11% of each run, Pallas kernels for 3% -> 3%
where the time goes in v3:
time: 465 us; the launch traced here: 457 us
  Pallas kernels  257 us (55%)
  matrix products  87.8 us (19%)
  local copies, waits for them, and re-layouts  52.1 us (11%)
  other arithmetic  45 us (10%)
  between operations  15.7 us (3%)
    pallas_call x1, Pallas kernels, back(): pl.pallas_call(functools.partial(back_kernel, parts, owners, plan), out_s...  160 us
    dot_general x7, matrix products, contract(): lax.dot_general(left, right, (((left_dim,), (right_dim,)), ((), ())), pre...  67.9 us
    pallas_call x1, Pallas kernels, front(): pl.pallas_call(functools.partial(front_kernel, parts, owners), out_shape=...  57.2 us
    pallas_call x3, Pallas kernels, exchange(): pl.pallas_call(functools.partial(exchange_kernel, parts, owners, kinds),...  39.7 us
    dot_general x1, matrix products, body(): jnp.dot(features, first_low, preferred_element_type=jnp.float32)  13.1 us
    convert_element_type x1, other arithmetic, body(): (mish_slope(linear_two) * outgoing_two).astype(jnp.bfloat16)  12.9 us
    unnamed x67, local copies, waits for them, and re-layouts  12.8 us
  transfers between devices with their start and end apart: 1, of which 0 were waited for; matrix products, arithmetic and copies ran while one was open for 11% of the time, Pallas kernels for 3%

profile of v3, /device:TPU:0, one launch (start us, length us, event | category | flops | bytes accessed | tf_op | source)
XLA Modules:
  0.0 457.4 jit_solution(16313930281673639862)
XLA Ops:
  7.2 1.0 convert_element_type.78
  8.4 3.0 add_convert_fusion.2
  11.3 0.8 convert_bitcast_fusion.1
  12.2 0.8 subtract_select_fusion
  13.1 1.4 convert_bitcast_fusion
  14.5 6.4 %reshape.233 = bf16[450,4,450]{2,1,0:T(4,128)(2,1)} reshape(bf16[450,1800]{1,0:T(8,128)(2,1)} %convert_bitcast_fusion) | data formatting | bytes 3240000 | tf_op jit(solution)/shard_map/reshape | solution.py:813
  20.9 2.3 pad.35
  23.2 1.9 copy.120
  25.1 57.2 %front.1 = (bf16[1024,2048]{1,0:T(8,128)(2,1)S(1)}, bf16[1024,1024]{1,0:T(8,128)(2,1)S(1)}, f32[4,8,512]{2,1,0:T(8,128)S(1)}, bf16[4,32,512]{2,1,0:T(8,128)(2,1)S(1)}, s32[8,1,1024]{2,1,0:T(1,128)S(1)}) custom-call(bf16[128,512]{1,0:T(8,128)(2,1)S(1)} %pad.32.first, bf16[4,1024,256]{2,1,0:T(8,128)(2,1)S(1)} %bitcast.120, f32[8,512]{1,0:T(8,128)S(1)} %pad.33.norms, ...), custom_call_target="tpu_custom_call" | custom-call | tf_op jit(solution)/shard_map/front/pallas_call | solution.py:261
  82.4 1.3 copy-done
  83.7 1.9 copy-done.2
  85.7 0.8 copy.105
  86.5 3.4 convert_reduce_fusion
  90.6 13.2 %subtract_convert_fusion = (bf16[32,2048]{1,0:T(8,128)(2,1)S(1)}, bf16[32,2048]{1,0:T(8,128)(2,1)S(1)}) fusion(bf16[8192,32]{0,1:T(8,128)(2,1)S(1)} %copy-done.28, s32[8192]{0:T(1024)S(1)} %fusion.23), kind=kOutput, calls=%fused_computation.45 | convolution fusion | flops 1090846720 | bytes 819200 | tf_op jit(solution)/shard_map/dot_general | solution.py:41
  104.6 2.5 copy.97
  107.1 13.1 %multiply_reduce_fusion.1 = (f32[2048]{0:T(1024)S(1)}, f32[2048]{0:T(1024)S(1)}, f32[1024,2048]{1,0:T(8,128)}, f32[1024,2048]{1,0:T(8,128)}) fusion(f32[1024]{0:T(1024)S(1)} %convert_reduce_fusion, bf16[1024,1024]{1,0:T(8,128)(2,1)S(1)} %copy-done.1, bf16[1024,2048]{1,0:T(8,128)(2,1)} %copy-done.2), kind=kOutput, calls=%fused_computation.14 | convolution fusion | flops 4318031872 | bytes 23089152 | tf_op jit(solution)/shard_map/dot_general | solution.py:838
  120.2 1.3 select_maximum_fusion.3.refs_0_
  121.6 15.2 %exchange.3 = (f32[40,128]{1,0:T(8,128)}, bf16[8,64,256]{2,1,0:T(8,128)(2,1)}) custom-call(f32[40,128]{1,0:T(8,128)} %select_maximum_fusion.3.refs_0_, bf16[8,64,256]{2,1,0:T(8,128)(2,1)} %bitcast.133), custom_call_target="tpu_custom_call" | custom-call | tf_op jit(solution)/shard_map/exchange/pallas_call | solution.py:159
  136.8 1.2 slice.72
  138.0 1.0 copy.116
  139.0 6.8 %fusion.2 = f32[64,4096]{1,0:T(8,128)S(1)} fusion(bf16[64,2048]{1,0:T(8,128)(2,1)S(1)} %bitcast.141, s32[2048]{0:T(1024)S(1)} %bitcast.165), kind=kOutput, calls=%fused_computation.4 | convolution fusion | flops 1082130432 | bytes 1318912 | tf_op jit(solution)/shard_map/dot_general | solution.py:854
  148.1 1.0 copy.100.refs_7_
  149.7 0.8 copy.103
  150.5 0.8 copy.102
  152.8 19.7 %multiply_reduce_fusion = (f32[2048]{0:T(1024)S(1)}, f32[2048]{0:T(1024)S(1)}, f32[1024,2048]{1,0:T(8,128)}, f32[1024,2048]{1,0:T(8,128)}) fusion(f32[1024]{0:T(1024)S(1)} %convert_reduce_fusion, bf16[2048,2048]{1,0:T(8,128)(2,1)} %all-gather.2.cloned.1.call-done.refs_3_, f32[1024,2048]{1,0:T(8,128)} %get-tuple-element.163, f32[2048]{0:T(1024)S(1)} %bitcast.171, ...), kind=kOutput, calls=%fused_computation.12 | convolution fusion | flops 8623484928 | bytes 33607680 | tf_op jit(solution)/shard_map/dot_general | solution.py:41
  173.1 11.2 %exchange.4 = (f32[32,128]{1,0:T(8,128)}, f32[4,32,1024]{2,1,0:T(8,128)}) custom-call(f32[32,128]{1,0:T(8,128)} %pad_maximum_fusion.1.refs_0_, f32[4,32,1024]{2,1,0:T(8,128)} %bitcast.131), custom_call_target="tpu_custom_call" | custom-call | tf_op jit(solution)/shard_map/exchange/pallas_call | solution.py:159
  184.3 1.3 divide_bitcast_fusion
  185.7 1.4 fusion.31
  187.1 1.1 reduce_sum.86
  188.2 5.8 %convert_reduce_fusion.1 = (f32[32]{0:T(128)S(1)}, bf16[32,1024]{1,0:T(8,128)(2,1)S(1)}, bf16[32,1024]{1,0:T(8,128)(2,1)}) fusion(f32[32,1024]{1,0:T(8,128)S(1)} %reduce_sum.86, f32[1024]{0:T(1024)S(1)} %get-tuple-element.176, f32[32]{0:T(128)S(1)} %copy-done.24, bf16[32,2048]{1,0:T(8,128)(2,1)S(1)} %bitcast.135, f32[1024,2048]{1,0:T(8,128)} %get-tuple-element.157, ...), kind=kOutput, calls=%fused_computation.47 | convolution fusion | flops 144932832 | bytes 8818944 | tf_op jit(solution)/shard_map/dot_general | solution.py:41
  193.9 4.2 multiply_reduce_fusion.2
  198.1 1.5 fusion.18
  200.3 13.3 %exchange.5 = (f32[40,128]{1,0:T(8,128)}, bf16[4,32,1024]{2,1,0:T(8,128)(2,1)}) custom-call(f32[40,128]{1,0:T(8,128)} %select_maximum_fusion.2.refs_0_, bf16[32,1024]{1,0:T(8,128)(2,1)} %get-tuple-element.164.refs_1_), custom_call_target="tpu_custom_call" | custom-call | tf_op jit(solution)/shard_map/exchange/pallas_call | solution.py:159
  213.5 1.3 fusion.48
  214.8 12.9 %multiply_convert_fusion.refs_2_ = bf16[1024,2048]{1,0:T(8,128)(2,1)S(1)} fusion(f32[1024,2048]{1,0:T(8,128)} %get-tuple-element.180, f32[1024,2048]{1,0:T(8,128)} %get-tuple-element.178, f32[1024,2048]{1,0:T(8,128)} %get-tuple-element.157, f32[]{:T(128)} %bitcast.11, f32[2048]{0:T(1024)S(1)} %get-tuple-element.170, f32[2048]{0:T(1024)S(1)} %get-tuple-element.171, ...), kind=kLoop, calls=%fused_computation.17 | loop fusion | flops 52428800 | bytes 29405188 | tf_op jit(solution)/shard_map/convert_element_type | solution.py:894
  227.8 16.6 %fusion.16 = f32[2048,2048]{1,0:T(8,128)} fusion(bf16[1024,2048]{1,0:T(8,128)(2,1)S(1)} %multiply_convert_fusion.refs_2_, f32[1024,2048]{1,0:T(8,128)} %get-tuple-element.163, f32[2048]{0:T(1024)S(1)} %bitcast.172, f32[2048]{0:T(1024)S(1)} %get-tuple-element.158, f32[2048]{0:T(1024)S(1)} %bitcast.149, f32[2048]{0:T(1024)S(1)} %bitcast.159), kind=kOutput, calls=%fused_computation.50 | convolution fusion | flops 8600420352 | bytes 29392896 | tf_op jit(solution)/shard_map/dot_general | solution.py:41
  244.4 1.0 pad.38.refs_1_
  245.5 6.9 %fusion.14 = bf16[32,2048]{1,0:T(8,128)(2,1)S(1)} fusion(bf16[32,4096]{1,0:T(8,128)(2,1)S(1)} %bitcast.143, s32[2048]{0:T(1024)S(1)} %bitcast.166), kind=kOutput, calls=%fused_computation.34 | convolution fusion | flops 545325056 | bytes 401408 | tf_op jit(solution)/shard_map/dot_general | solution.py:41
  253.0 159.8 %back.1 = (f32[4,2,64,2048]{3,2,1,0:T(8,128)}, f32[4,2,64,128]{3,2,1,0:T(8,128)}, f32[128,512]{1,0:T(8,128)}, bf16[4,32,2048]{2,1,0:T(8,128)(2,1)}, f32[32,128]{1,0:T(8,128)}) custom-call(f32[4,512,2048]{2,1,0:T(8,128)} %bitcast.124, f32[4,512,128]{2,1,0:T(8,128)} %pad.38.refs_1_, bf16[1024,2048]{1,0:T(8,128)(2,1)} %copy-done.4, ...), custom_call_target="tpu_custom_call" | custom-call | tf_op jit(solution)/shard_map/back/pallas_call | solution.py:723
  412.8 1.9 copy.119
  414.7 1.4 fusion.44
  419.4 4.3 slice.95
  423.7 5.7 %reshape.253 = f32[450,4,512]{2,1,0:T(4,128)} reshape(f32[450,2048]{1,0:T(8,128)} %slice.95) | data formatting | bytes 7372800 | tf_op jit(solution)/shard_map/reshape | solution.py:917
  429.4 6.0 %reshape.254 = f32[450,1800]{1,0:T(8,128)} reshape(f32[450,4,450]{2,1,0:T(4,128)} %bitcast.125) | data formatting | bytes 6480000 | tf_op jit(solution)/shard_map/reshape | solution.py:918
  435.4 1.6 slice.97
  437.0 1.7 copy.112
  438.7 1.2 multiply_subtract_fusion.4
  440.0 8.5 %fusion.41 = (bf16[1800,450]{0,1:T(8,128)(2,1)}, f32[1800,450]{0,1:T(8,128)}, f32[1800,450]{0,1:T(8,128)}, f32[1800,450]{0,1:T(8,128)}) fusion(f32[1800,450]{0,1:T(8,128)S(1)} %copy-done.6, f32[450,1800]{1,0:T(8,128)} %reshape.254, f32[1800,450]{0,1:T(8,128)} %param.33, f32[1800,450]{0,1:T(8,128)} %param.32), kind=kLoop, calls=%fused_computation.112 | loop fusion | flops 12960000 | bytes 24300000 | tf_op jit(solution)/shard_map/convert_element_type | solution.py:947
  (91 shorter events, 11.9 us)
Async XLA Ops:
  7.2 145.6 %all-gather.2.cloned.1.call-start = ((), (), s32[]{:S(2)}) async-start(), calls=%async_computation | async-start | bytes 10485760 | tf_op jit(solution)/shard_map/all_gather | solution.py:817
  8.4 4.7 %copy-start.5 = (f32[1800,450]{0,1:T(8,128)S(1)}, f32[1800,450]{0,1:T(8,128)}, u32[]{:S(2)}) copy-start(f32[1800,450]{0,1:T(8,128)} %param.26) | copy-start | bytes 9720004
  13.1 12.1 %copy-start.16 = (f32[4,450]{1,0:T(4,128)S(1)}, f32[4,450]{1,0:T(4,128)}, u32[]{:S(2)}) copy-start(f32[4,450]{1,0:T(4,128)} %param.28) | copy-start | bytes 21604
  14.5 71.2 %copy-start.7 = (f32[128,450]{0,1:T(8,128)S(1)}, f32[128,450]{0,1:T(8,128)}, u32[]{:S(2)}) copy-start(f32[128,450]{0,1:T(8,128)} %param.25) | copy-start | bytes 691204
  14.5 76.1 %copy-start.15 = (s32[8192]{0:T(1024)S(1)}, s32[8192]{0:T(1024)}, u32[]{:S(2)}) copy-start(s32[8192]{0:T(1024)} %param.23) | copy-start | bytes 98308
  14.5 76.1 %copy-start.28 = (bf16[8192,32]{0,1:T(8,128)(2,1)S(1)}, bf16[8192,32]{0,1:T(8,128)(2,1)}, u32[]{:S(2)}) copy-start(bf16[8192,32]{0,1:T(8,128)(2,1)} %param.24) | copy-start | bytes 1572868
  82.4 1.3 copy-start
  83.7 1.9 copy-start.2
  90.6 14.0 %copy-start.1 = (bf16[1024,1024]{1,0:T(8,128)(2,1)S(1)}, bf16[1024,1024]{1,0:T(8,128)(2,1)}, u32[]{:S(2)}) copy-start(bf16[1024,1024]{1,0:T(8,128)(2,1)} %copy-done) | copy-start | bytes 6291460
  120.2 29.5 %copy-start.11 = (f32[128,450]{0,1:T(8,128)S(1)}, f32[128,450]{0,1:T(8,128)}, u32[]{:S(2)}) copy-start(f32[128,450]{0,1:T(8,128)} %param.31) | copy-start | bytes 691204
  120.2 30.3 %copy-start.12 = (f32[128,450]{0,1:T(8,128)S(1)}, f32[128,450]{0,1:T(8,128)}, u32[]{:S(2)}) copy-start(f32[128,450]{0,1:T(8,128)} %param.30) | copy-start | bytes 691204
  138.0 13.4 %copy-start.21 = (f32[40,128]{1,0:T(8,128)S(1)}, f32[40,128]{1,0:T(8,128)}, u32[]{:S(2)}) copy-start(f32[40,128]{1,0:T(8,128)} %get-tuple-element.42) | copy-start | bytes 61444
  152.8 35.4 %copy-start.24 = (f32[32]{0:T(128)S(1)}, f32[32]{0:T(128)}, u32[]{:S(2)}) copy-start(f32[32]{0:T(128)} %param.29) | copy-start | bytes 388
  188.1 5.8 %copy-start.3 = (f32[1024,2048]{1,0:T(8,128)S(1)}, f32[1024,2048]{1,0:T(8,128)}, u32[]{:S(2)}) copy-start(f32[1024,2048]{1,0:T(8,128)} %get-tuple-element.157) | copy-start | bytes 25165828
  227.8 16.6 %copy-start.4 = (bf16[1024,2048]{1,0:T(8,128)(2,1)}, bf16[1024,2048]{1,0:T(8,128)(2,1)S(1)}, u32[]{:S(2)}) copy-start(bf16[1024,2048]{1,0:T(8,128)(2,1)S(1)} %multiply_convert_fusion.refs_2_) | copy-start | bytes 12582916
  227.8 17.7 %copy-start.9 = (bf16[4,32,1024]{2,1,0:T(8,128)(2,1)S(1)}, bf16[4,32,1024]{2,1,0:T(8,128)(2,1)}, u32[]{:S(2)}) copy-start(bf16[4,32,1024]{2,1,0:T(8,128)(2,1)} %get-tuple-element.49) | copy-start | bytes 786436
  423.7 15.0 %copy-start.20 = (f32[32,128]{1,0:T(8,128)S(1)}, f32[32,128]{1,0:T(8,128)}, u32[]{:S(2)}) copy-start(f32[32,128]{1,0:T(8,128)} %get-tuple-element.54) | copy-start | bytes 49156
  423.7 15.0 %copy-start.25 = (f32[32]{0:T(128)S(1)}, f32[32]{0:T(128)}, u32[]{:S(2)}) copy-start(f32[32]{0:T(128)} %param.29) | copy-start | bytes 388
  423.7 15.0 %copy-start.26 = (f32[32]{0:T(128)S(1)}, f32[32]{0:T(128)}, u32[]{:S(2)}) copy-start(f32[32]{0:T(128)} %param.39) | copy-start | bytes 388
  423.7 15.0 %copy-start.27 = (f32[32]{0:T(128)S(1)}, f32[32]{0:T(128)}, u32[]{:S(2)}) copy-start(f32[32]{0:T(128)} %param.38) | copy-start | bytes 388
  423.7 16.3 %copy-start.6 = (f32[1800,450]{0,1:T(8,128)S(1)}, f32[1800,450]{0,1:T(8,128)}, u32[]{:S(2)}) copy-start(f32[1800,450]{0,1:T(8,128)} %param.26) | copy-start | bytes 9720004
  439.9 8.6 %copy-start.8 = (f32[450,32]{0,1:T(8,128)S(1)}, f32[450,32]{0,1:T(8,128)}, u32[]{:S(2)}) copy-start(f32[450,32]{0,1:T(8,128)} %param.27) | copy-start | bytes 172804
  439.9 8.6 %copy-start.10 = (f32[450,32]{0,1:T(8,128)S(1)}, f32[450,32]{0,1:T(8,128)}, u32[]{:S(2)}) copy-start(f32[450,32]{0,1:T(8,128)} %copy.112) | copy-start | bytes 172804
  439.9 8.6 %copy-start.13 = (f32[450,32]{0,1:T(8,128)S(1)}, f32[450,32]{0,1:T(8,128)}, u32[]{:S(2)}) copy-start(f32[450,32]{0,1:T(8,128)} %param.35) | copy-start | bytes 172804
  440.0 8.6 %copy-start.14 = (f32[450,32]{0,1:T(8,128)S(1)}, f32[450,32]{0,1:T(8,128)}, u32[]{:S(2)}) copy-start(f32[450,32]{0,1:T(8,128)} %param.34) | copy-start | bytes 172804
  440.0 9.3 %copy-start.17 = (f32[4,450]{1,0:T(4,128)S(1)}, f32[4,450]{1,0:T(4,128)}, u32[]{:S(2)}) copy-start(f32[4,450]{1,0:T(4,128)} %param.28) | copy-start | bytes 21604
  440.0 9.3 %copy-start.18 = (f32[16,128]{1,0:T(8,128)S(1)}, f32[16,128]{1,0:T(8,128)}, u32[]{:S(2)}) copy-start(f32[16,128]{1,0:T(8,128)} %get-tuple-element.169) | copy-start | bytes 24580
  440.0 9.3 %copy-start.19 = (f32[16,128]{1,0:T(8,128)S(1)}, f32[16,128]{1,0:T(8,128)}, u32[]{:S(2)}) copy-start(f32[16,128]{1,0:T(8,128)} %get-tuple-element.172) | copy-start | bytes 24580
  440.0 9.3 %copy-start.22 = (f32[4,450]{1,0:T(4,128)S(1)}, f32[4,450]{1,0:T(4,128)}, u32[]{:S(2)}) copy-start(f32[4,450]{1,0:T(4,128)} %param.37) | copy-start | bytes 21604
  440.0 9.3 %copy-start.23 = (f32[4,450]{1,0:T(4,128)S(1)}, f32[4,450]{1,0:T(4,128)}, u32[]{:S(2)}) copy-start(f32[4,450]{1,0:T(4,128)} %param.36) | copy-start | bytes 21604
Sparse Core Ops, SparseCore 0:
  85.8 56.9 all-gather.1
